TPU v7x, 32 devices: a whole 2x2x4 slice. The times are simulated.
32 devices in a mesh: ctx: 8 (over z, x), fsdp: 4 (over y, core).
Axes of the slice: x: 2, y: 2, z: 4, core: 2. Of those that a mesh axis runs over, the one named last changes fastest.
Arguments:
- inputs: bfloat16 [4, 1024, 1024], P('fsdp', 'ctx'), may hold values from -6 to 6
- segment_ids: int32 [4, 1024], P('fsdp', 'ctx'), may hold values from 0 to 1, never falling along the last dimension, each value on 1 to 768 neighbouring positions
- gain_attn: bfloat16 [1024], P(('ctx', 'fsdp')), may hold values from 0.5 to 1.5
- w_qkv: bfloat16 [1024, 3072], P(('ctx', 'fsdp')), may hold values from -4 to 4
- w_out_attn: bfloat16 [1024, 1024], P(('ctx', 'fsdp')), may hold values from -1.5 to 1.5
- gain_mlp: bfloat16 [1024], P(('ctx', 'fsdp')), may hold values from 0.5 to 1.5
- w_in: bfloat16 [1024, 5248], P(('ctx', 'fsdp')), may hold values from -0.1875 to 0.1875
- w_out_mlp: bfloat16 [2624, 1024], P(None, ('ctx', 'fsdp')), may hold values from -0.125 to 0.125
- cotangent: bfloat16 [4, 1024, 1024], P('fsdp', 'ctx'), may hold values from -6 to 6
Outputs:
- block_out: bfloat16 [4, 1024, 1024], P('fsdp', 'ctx')
- grad_input: bfloat16 [4, 1024, 1024], P('fsdp', 'ctx')
- grad_w_qkv: float32 [1024, 3072], P(('ctx', 'fsdp'))
- grad_w_out_attn: float32 [1024, 1024], P(('ctx', 'fsdp'))
- grad_w_in: float32 [1024, 5248], P(('ctx', 'fsdp'))
- grad_w_out_mlp: float32 [2624, 1024], P(None, ('ctx', 'fsdp'))
- grad_gain_attn: float32 [1024], P(('ctx', 'fsdp'))
- grad_gain_mlp: float32 [1024], P(('ctx', 'fsdp'))
Inputs may be any that keep to these rules, and one draw needn't show every extreme that they name: `segment_ids`: along a row the ids never fall: segment 0 comes first, then segment 1; each segment holds 256 to 768 tokens.
All inputs are finite; a program needn't handle non-finite values.
Results may differ from a plain program's by a relative error of at most 0.015.
Values may be sent and summed in bfloat16 or wider, within the bound.
A program may use at most 256 MiB of HBM per device.

v0:
```python
import math

import jax
import jax.numpy as jnp
from jax import lax
from jax.sharding import PartitionSpec as P

HEADS = 16
HD = 64


EPSILON = 1e-05
ROPE_BASE = 160000.0
MASKED = -1e30


def layer_norm(values):
    center = values - jnp.mean(values, axis=-1, keepdims=True)
    scaled = lax.rsqrt(jnp.mean(center * center, axis=-1, keepdims=True) + EPSILON)
    return (center * scaled, scaled)


def norm_back(grad_norm, normed, scaled):
    return scaled * (
        grad_norm
        - jnp.mean(grad_norm, axis=-1, keepdims=True)
        - normed * jnp.mean(grad_norm * normed, axis=-1, keepdims=True)
    )


def rope_columns(positions, head_size):
    freqs = ROPE_BASE ** (-jnp.arange(0, head_size, 2, dtype=jnp.float32) / head_size)
    angles = freqs[:, None] * positions[None, :]
    cosine = jnp.concatenate([jnp.cos(angles), jnp.cos(angles)], axis=0)
    sine = jnp.concatenate([jnp.sin(angles), jnp.sin(angles)], axis=0)
    return (cosine[None], sine[None])


def rotate_cols(values, cosine, sine):
    half = values.shape[1] // 2
    turned = jnp.concatenate([-values[:, half:], values[:, :half]], axis=1)
    return values * cosine + turned * sine


def unrotate_cols(grads, cosine, sine):
    half = grads.shape[1] // 2
    weighted = grads * sine
    turned = jnp.concatenate([weighted[:, half:], -weighted[:, :half]], axis=1)
    return grads * cosine + turned


def gelu_slope(values):
    return (
        0.5 * (1.0 + lax.erf(values * 0.7071067811865476))
        + values * jnp.exp(-0.5 * values * values) * 0.3989422804014327
    )


def block_scores(query_part, key_part, seg_query, seg_key, scale):
    scores = (
        jnp.einsum("hdt,hds->hts", query_part, key_part, preferred_element_type=jnp.float32) * scale
    )
    return jnp.where((seg_query[:, None] == seg_key[None, :])[None], scores, MASKED)


def pair_grads(
    query_part, key_part, value_part, grad_part, seg_query, seg_key, log_part, dots_part, scale
):
    scores = block_scores(query_part, key_part, seg_query, seg_key, scale)
    block_probs = jnp.exp(scores - log_part)
    block_half = block_probs.astype(jnp.bfloat16)
    grad_probs = jnp.einsum(
        "hdt,hds->hts", grad_part, value_part, preferred_element_type=jnp.float32
    )
    grad_scores = (block_probs * (grad_probs - dots_part)).astype(jnp.bfloat16)
    return (grad_scores, block_half)


def to_blocks(values, heads, head_size, block_count, block_size):
    return jnp.transpose(values.reshape(heads, head_size, block_count, block_size), (2, 0, 1, 3))


def body(inputs, segment_ids, gain_attn, w_qkv, w_out_attn, gain_mlp, w_in, w_out_mlp, cotangent):
    tokens = inputs[0].astype(jnp.float32)
    tok_count, width = tokens.shape
    heads = HEADS
    head_size = HD
    scale = 1.0 / math.sqrt(head_size)
    qkv_full, attn_full, in_full, mlp_full, gain_one, gain_two = (
        lax.all_gather(w_qkv, ("ctx", "fsdp"), axis=0, tiled=True),
        lax.all_gather(w_out_attn, ("ctx", "fsdp"), axis=0, tiled=True),
        lax.all_gather(w_in, ("ctx", "fsdp"), axis=0, tiled=True),
        lax.all_gather(w_out_mlp, ("ctx", "fsdp"), axis=1, tiled=True),
        lax.all_gather(gain_attn, ("ctx", "fsdp"), axis=0, tiled=True),
        lax.all_gather(gain_mlp, ("ctx", "fsdp"), axis=0, tiled=True),
    )
    hidden_units = mlp_full.shape[0]
    gain_first = gain_one.astype(jnp.float32)
    gain_second = gain_two.astype(jnp.float32)
    normed_one, scale_one = layer_norm(tokens)
    normed_attn = (normed_one * gain_first).astype(jnp.bfloat16)
    projected_cols = jnp.einsum(
        "de,td->et", qkv_full, normed_attn, preferred_element_type=jnp.float32
    )
    positions = (lax.axis_index("ctx") * tok_count + jnp.arange(tok_count, dtype=jnp.int32)).astype(
        jnp.float32
    )
    cosine, sine = rope_columns(positions, head_size)
    query_cols = rotate_cols(
        projected_cols[:width].reshape(heads, head_size, tok_count), cosine, sine
    ).astype(jnp.bfloat16)
    key_cols = rotate_cols(
        projected_cols[width : 2 * width].reshape(heads, head_size, tok_count), cosine, sine
    ).astype(jnp.bfloat16)
    value_cols = projected_cols[2 * width :].astype(jnp.bfloat16)
    seg_own = segment_ids[0].astype(jnp.bfloat16)
    keys_all, values_all, seg_all = (
        lax.all_gather(key_cols.reshape(width, tok_count), "ctx", axis=1, tiled=True),
        lax.all_gather(value_cols, "ctx", axis=1, tiled=True),
        lax.all_gather(seg_own, "ctx", axis=0, tiled=True),
    )
    key_count = keys_all.shape[1]
    block_size = min(512, key_count)
    block_count = key_count // block_size
    key_blocks = to_blocks(keys_all, heads, head_size, block_count, block_size)
    value_blocks = to_blocks(values_all, heads, head_size, block_count, block_size)
    seg_blocks = seg_all.reshape(block_count, block_size)

    def totals_step(carry, pieces):
        peak, total = carry
        key_piece, seg_piece = pieces
        scores = block_scores(query_cols, key_piece, seg_own, seg_piece, scale)
        new_peak = jnp.maximum(peak, jnp.max(scores, axis=-1, keepdims=True))
        total = total * jnp.exp(peak - new_peak) + jnp.sum(
            jnp.exp(scores - new_peak), axis=-1, keepdims=True
        )
        return ((new_peak, total), None)

    start_peak = jnp.full((heads, tok_count, 1), MASKED, jnp.float32)
    start_total = jnp.zeros((heads, tok_count, 1), jnp.float32)
    (peak, total), unused = lax.scan(
        totals_step, (start_peak, start_total), (key_blocks, seg_blocks)
    )
    log_total = peak + jnp.log(total)

    def attend_step(acc, pieces):
        key_piece, value_piece, seg_piece = pieces
        scores = block_scores(query_cols, key_piece, seg_own, seg_piece, scale)
        probs_half = jnp.exp(scores - log_total).astype(jnp.bfloat16)
        return (
            acc
            + jnp.einsum(
                "hts,hds->hdt", probs_half, value_piece, preferred_element_type=jnp.float32
            ),
            None,
        )

    zero_cols = jnp.zeros((heads, head_size, tok_count), jnp.float32)
    attended_sum, unused = lax.scan(attend_step, zero_cols, (key_blocks, value_blocks, seg_blocks))
    attended_cols = attended_sum.astype(jnp.bfloat16)
    attended = attended_cols.reshape(width, tok_count).T
    residual = tokens + jnp.dot(attended, attn_full, preferred_element_type=jnp.float32)
    normed_two, scale_two = layer_norm(residual)
    normed_mlp = (normed_two * gain_second).astype(jnp.bfloat16)
    expanded = jnp.dot(normed_mlp, in_full, preferred_element_type=jnp.float32)
    pre_act = expanded[:, :hidden_units]
    gate_part = expanded[:, hidden_units:]
    activated = jax.nn.gelu(pre_act, approximate=False)
    product = (activated * gate_part).astype(jnp.bfloat16)
    block_out = (residual + jnp.dot(product, mlp_full, preferred_element_type=jnp.float32)).astype(
        jnp.bfloat16
    )
    grad_out = cotangent[0]
    grad_product = jnp.einsum("td,fd->tf", grad_out, mlp_full, preferred_element_type=jnp.float32)
    grad_expanded = jnp.concatenate(
        [grad_product * gate_part * gelu_slope(pre_act), grad_product * activated], axis=1
    ).astype(jnp.bfloat16)
    normed_part = normed_mlp
    mlp_rows = lax.psum_scatter(
        jnp.concatenate(
            [
                jnp.einsum(
                    "td,tf->df", normed_part, grad_expanded, preferred_element_type=jnp.float32
                ),
                jnp.einsum("td,tf->df", grad_out, product, preferred_element_type=jnp.float32),
            ],
            axis=1,
        ),
        ("ctx", "fsdp"),
        scatter_dimension=0,
        tiled=True,
    )
    grad_normed_mlp = jnp.einsum(
        "tf,df->td", grad_expanded, in_full, preferred_element_type=jnp.float32
    )
    grad_gain_two = jnp.sum(grad_normed_mlp * normed_two, axis=0)
    grad_residual = grad_out.astype(jnp.float32) + norm_back(
        grad_normed_mlp * gain_second, normed_two, scale_two
    )
    residual_half = grad_residual.astype(jnp.bfloat16)
    grad_attended = jnp.einsum(
        "te,de->dt", residual_half, attn_full, preferred_element_type=jnp.float32
    ).astype(jnp.bfloat16)
    grad_att_cols = grad_attended.reshape(heads, head_size, tok_count)
    row_dots = jnp.sum(
        grad_att_cols.astype(jnp.float32) * attended_cols.astype(jnp.float32), axis=1
    )[:, :, None]

    def key_block(grad_query_sum, pieces):
        key_piece, value_piece, seg_piece = pieces
        grad_scores, block_half = pair_grads(
            query_cols,
            key_piece,
            value_piece,
            grad_att_cols,
            seg_own,
            seg_piece,
            log_total,
            row_dots,
            scale,
        )
        grad_query_sum = grad_query_sum + jnp.einsum(
            "hts,hds->hdt", grad_scores, key_piece, preferred_element_type=jnp.float32
        )
        key_part = (
            jnp.einsum("hts,hdt->hds", grad_scores, query_cols, preferred_element_type=jnp.float32)
            * scale
        )
        value_part = jnp.einsum(
            "hts,hdt->hds", block_half, grad_att_cols, preferred_element_type=jnp.float32
        )
        return (grad_query_sum, (key_part, value_part))

    grad_query_sum, (key_parts, value_parts) = lax.scan(
        key_block, zero_cols, (key_blocks, value_blocks, seg_blocks)
    )
    key_terms = jnp.transpose(key_parts, (1, 2, 0, 3)).reshape(width, key_count)
    value_terms = jnp.transpose(value_parts, (1, 2, 0, 3)).reshape(width, key_count)
    grad_keys, grad_values = (
        lax.psum_scatter(
            key_terms.astype(jnp.bfloat16), "ctx", scatter_dimension=1, tiled=True
        ).astype(jnp.float32),
        lax.psum_scatter(
            value_terms.astype(jnp.bfloat16), "ctx", scatter_dimension=1, tiled=True
        ).astype(jnp.float32),
    )
    grad_key_cols = grad_keys.reshape(heads, head_size, tok_count)
    grad_query_rot = unrotate_cols(grad_query_sum * scale, cosine, sine).reshape(width, tok_count)
    grad_key_rot = unrotate_cols(grad_key_cols, cosine, sine).reshape(width, tok_count)
    grad_proj_cols = jnp.concatenate([grad_query_rot, grad_key_rot, grad_values], axis=0).astype(
        jnp.bfloat16
    )
    normed_part = normed_attn
    attn_rows = lax.psum_scatter(
        jnp.concatenate(
            [
                jnp.einsum(
                    "td,et->de", normed_part, grad_proj_cols, preferred_element_type=jnp.float32
                ),
                jnp.einsum(
                    "td,te->de", attended, residual_half, preferred_element_type=jnp.float32
                ),
            ],
            axis=1,
        ),
        ("ctx", "fsdp"),
        scatter_dimension=0,
        tiled=True,
    )
    grad_normed_attn = jnp.einsum(
        "de,et->td", qkv_full, grad_proj_cols, preferred_element_type=jnp.float32
    )
    grad_gain_one = jnp.sum(grad_normed_attn * normed_one, axis=0)
    grad_tokens = (
        grad_residual + norm_back(grad_normed_attn * gain_first, normed_one, scale_one)
    ).astype(jnp.bfloat16)
    gain_sum_one, gain_sum_two = (
        lax.psum_scatter(grad_gain_one, ("ctx", "fsdp"), scatter_dimension=0, tiled=True),
        lax.psum_scatter(grad_gain_two, ("ctx", "fsdp"), scatter_dimension=0, tiled=True),
    )
    grad_qkv_rows = attn_rows[:, : 3 * width]
    grad_attn_rows = attn_rows[:, 3 * width :]
    grad_in_rows = mlp_rows[:, : 2 * hidden_units]
    grad_mlp_cols = mlp_rows[:, 2 * hidden_units :].T
    return (
        block_out[None],
        grad_tokens[None],
        grad_qkv_rows,
        grad_attn_rows,
        grad_in_rows,
        grad_mlp_cols,
        gain_sum_one,
        gain_sum_two,
    )


def solution(mesh):
    in_specs = (
        P("fsdp", "ctx", None),
        P("fsdp", "ctx"),
        P(("ctx", "fsdp")),
        P(("ctx", "fsdp"), None),
        P(("ctx", "fsdp"), None),
        P(("ctx", "fsdp")),
        P(("ctx", "fsdp"), None),
        P(None, ("ctx", "fsdp")),
        P("fsdp", "ctx", None),
    )
    out_specs = (
        P("fsdp", "ctx", None),
        P("fsdp", "ctx", None),
        P(("ctx", "fsdp"), None),
        P(("ctx", "fsdp"), None),
        P(("ctx", "fsdp"), None),
        P(None, ("ctx", "fsdp")),
        P(("ctx", "fsdp")),
        P(("ctx", "fsdp")),
    )
    return jax.shard_map(body, mesh=mesh, in_specs=in_specs, out_specs=out_specs, check_vma=False)
```

profile of v0, /device:TPU:11, one launch (start us, length us, event | category | flops | bytes accessed | tf_op | source)
XLA Modules:
  0.0 1140.8 jit_solution(3911576453024629604)
XLA Ops:
  9.7 40.0 %all-reduce.5 = (bf16[1024]{0:T(1024)(128)(2,1)S(1)}, bf16[1024]{0:T(1024)(128)(2,1)S(1)}) all-reduce(bf16[1024]{0:T(1024)(128)(2,1)S(1)} %dynamic-update-slice, bf16[1024]{0:T(1024)(128)(2,1)S(1)} %dynamic-update-slice.1), channel_id=1, replica_groups=mesh['ctx'=8,'fsdp'=4] {'ctx','fsdp'}, use_global_device_ids=true, to_apply=%add | all-reduce | flops 2048 | bytes 8192
  51.9 30.1 %all-gather.8.cloned.1.call-done = bf16[1024,3072]{1,0:T(8,128)(2,1)} async-done(((bf16[32,3072]{1,0:T(8,128)(2,1)}), bf16[1024,3072]{1,0:T(8,128)(2,1)}) %all-gather.8.cloned.1.call-update) | async-done | bytes 6291472 | tf_op jit(solution)/shard_map/all_gather | solution.py:90
  82.0 3.9 convolution_bitcast_fusion.1
  91.1 11.3 all-gather
  102.9 29.3 %all-gather.10.cloned.1.call-done = bf16[1024,1024]{0,1:T(8,128)(2,1)} async-done(((bf16[1024,128]{0,1:T(8,128)(2,1)}), bf16[1024,1024]{0,1:T(8,128)(2,1)}) %all-gather.10.cloned.1.call-update) | async-done | bytes 2097168 | tf_op jit(solution)/shard_map/all_gather | solution.py:119
  137.8 3.4 copy.72
  141.2 41.3 %all-gather.12.cloned.1.call-done = bf16[1024,1024]{0,1:T(8,128)(2,1)} async-done(((bf16[1024,128]{0,1:T(8,128)(2,1)}), bf16[1024,1024]{0,1:T(8,128)(2,1)}) %all-gather.12.cloned.1.call-update) | async-done | bytes 2097168 | tf_op jit(solution)/shard_map/all_gather | solution.py:118
  190.3 4.2 while.39
  194.5 7.9 while.40
  194.7 3.7 fusion.148
  198.6 3.8 fusion.148
  204.2 37.2 %all-gather.14.cloned.1.call-done = bf16[1024,1024]{1,0:T(8,128)(2,1)} async-done(((bf16[32,1024]{1,0:T(8,128)(2,1)}), bf16[1024,1024]{1,0:T(8,128)(2,1)}) %all-gather.14.cloned.1.call-update) | async-done | bytes 2097168 | tf_op jit(solution)/shard_map/all_gather | solution.py:91
  243.8 87.4 %all-gather.16.cloned.1.call-done = bf16[1024,5248]{1,0:T(8,128)(2,1)} async-done(((bf16[32,5248]{1,0:T(8,128)(2,1)}), bf16[1024,5248]{1,0:T(8,128)(2,1)}) %all-gather.16.cloned.1.call-update) | async-done | bytes 10747920 | tf_op jit(solution)/shard_map/all_gather | solution.py:92
  331.3 7.2 fusion.98
  338.5 60.8 %all-gather.18.cloned.1.call-done = bf16[2624,1024]{0,1:T(8,128)(2,1)} async-done(((bf16[2624,32]{0,1:T(8,128)(2,1)}), bf16[2624,1024]{0,1:T(8,128)(2,1)}) %all-gather.18.cloned.1.call-update) | async-done | bytes 5373968 | tf_op jit(solution)/shard_map/all_gather | solution.py:93
  399.3 9.2 multiply_convert_fusion
  408.6 3.7 multiply_reduce_fusion
  417.9 18.3 %while.41 = (s32[]{:T(128)}, f32[16,64,128]{2,1,0:T(8,128)S(1)}, bf16[2,16,64,512]{3,2,1,0:T(8,128)(2,1)}, bf16[2,16,64,512]{3,2,1,0:T(8,128)(2,1)}, bf16[2,16,6...) while((s32[]{:T(128)}, f32[16,64,128]{2,1,0:T(8,128)S(1)}, ...), condition=%wide.region_14.15_spmd.clone, body=%wide.region_13.14_spmd.clone.sunk | while | flops 682426368 | bytes 71560816 | solution.py:234
  436.2 6.2 copy.94
  442.4 6.5 reshape.217
  450.4 4.8 copy.95
  455.2 6.5 reshape.218
  465.5 47.9 %reduce-scatter.13.cloned.1.call-done = bf16[128,1024]{1,0:T(8,128)(2,1)} async-done(((bf16[1024,1024]{1,0:T(8,128)(2,1)}), bf16[128,1024]{1,0:T(8,128)(2,1)}) %reduce-scatter.13.cloned.1.call-update) | async-done | bytes 262160
  514.8 69.5 %reduce-scatter.15.cloned.1.call-done = bf16[128,1024]{1,0:T(8,128)(2,1)} async-done(((bf16[1024,1024]{1,0:T(8,128)(2,1)}), bf16[128,1024]{1,0:T(8,128)(2,1)}) %reduce-scatter.15.cloned.1.call-update) | async-done | bytes 262160
  587.6 6.1 pad_maximum_fusion.1
  596.0 5.7 convolution_bitcast_fusion
  604.8 15.2 %pad_maximum_fusion = f32[1024,7872]{1,0:T(8,128)} fusion(f32[1024,2624]{1,0:T(8,128)} %convolution_bitcast_fusion, f32[1024,5248]{1,0:T(8,128)S(1)} %fusion.62), kind=kLoop, calls=%fused_computation.55 | loop fusion | flops 8060928 | bytes 64487424 | tf_op jit(solution)/shard_map/concatenate | solution.py:180
  620.1 5.2 fusion.61
  625.3 5.1 fusion.77
  630.5 44.2 %all-reduce.4 = (f32[1024]{0:T(1024)S(1)}, f32[1024]{0:T(1024)S(1)}) all-reduce(f32[1024]{0:T(1024)S(1)} %get-tuple-element.316, f32[1024]{0:T(1024)S(1)} %get-tuple-element.314), channel_id=7, replica_groups=mesh['ctx'=8,'fsdp'=4] {'ctx','fsdp'}, use_global_device_ids=true, to_apply=%region_22.23.clone | all-reduce | flops 2048 | bytes 16384
  676.8 103.4 %reduce-scatter.9.cloned.1.call-done = f32[32,4096]{1,0:T(8,128)} async-done(((f32[1024,4096]{1,0:T(8,128)}), f32[32,4096]{1,0:T(8,128)}) %reduce-scatter.9.cloned.1.call-update) | async-done | bytes 524304 | tf_op jit(solution)/shard_map/reduce_scatter | solution.py:254
  783.5 346.3 %reduce-scatter.11.cloned.1.call-done = f32[32,7872]{1,0:T(8,128)} async-done(((f32[1024,7872]{1,0:T(8,128)}), f32[32,7872]{1,0:T(8,128)}) %reduce-scatter.11.cloned.1.call-update) | async-done | bytes 1007632 | tf_op jit(solution)/shard_map/reduce_scatter | solution.py:179
  (188 shorter events, 80.2 us)
Async XLA Ops:
  7.2 74.8 %all-gather.8.cloned.1.call-start = ((), (), s32[]{:S(2)}) async-start(), calls=%async_computation.4 | async-start | bytes 6488064 | tf_op jit(solution)/shard_map/all_gather | solution.py:90
  7.9 124.3 %all-gather.10.cloned.1.call-start = ((), (), s32[]{:S(2)}) async-start(), calls=%async_computation.5 | async-start | bytes 2359296 | tf_op jit(solution)/shard_map/all_gather | solution.py:119
  86.7 95.8 %all-gather.12.cloned.1.call-start = ((), (), s32[]{:S(2)}) async-start(), calls=%async_computation.6 | async-start | bytes 2359296 | tf_op jit(solution)/shard_map/all_gather | solution.py:118
  88.4 2.7 copy-start.23
  89.3 152.1 %all-gather.14.cloned.1.call-start = ((), (), s32[]{:S(2)}) async-start(), calls=%async_computation.7 | async-start | bytes 2162688 | tf_op jit(solution)/shard_map/all_gather | solution.py:91
  89.9 241.4 %all-gather.16.cloned.1.call-start = ((), (), s32[]{:S(2)}) async-start(), calls=%async_computation.8 | async-start | bytes 11083776 | tf_op jit(solution)/shard_map/all_gather | solution.py:92
  90.4 308.9 %all-gather.18.cloned.1.call-start = ((), (), s32[]{:S(2)}) async-start(), calls=%async_computation.9 | async-start | bytes 5677056 | tf_op jit(solution)/shard_map/all_gather | solution.py:93
  91.0 422.4 %reduce-scatter.13.cloned.1.call-start = ((), (), s32[]{:S(2)}) async-start(), calls=%async_computation.12 | async-start | bytes 2359296
  202.4 39.0 %copy-start.21 = (f32[16,128,1]{1,0,2:T(8,128)}, f32[16,128,1]{1,0,2:T(8,128)S(1)}, u32[]{:S(2)}) copy-start(f32[16,128,1]{1,0,2:T(8,128)S(1)} %get-tuple-element.724) | copy-start | bytes 24580
  399.3 9.2 copy-start
  408.5 3.7 copy-start.16
  408.5 3.7 copy-start.18
  408.5 3.8 copy-start.14
  408.6 4.8 copy-start.3
  418.1 1.6 copy-start.12
  418.1 1.6 copy-start.13
  418.1 1.6 copy-start.22
  419.7 1.6 copy-start.7
  422.6 2.4 copy-start.10
  427.2 1.6 copy-start.12
  427.2 1.6 copy-start.13
  428.8 1.6 copy-start.7
  431.7 2.3 copy-start.10
  448.8 1.6 copy-start.9
  448.9 135.4 %reduce-scatter.15.cloned.1.call-start = ((), (), s32[]{:S(2)}) async-start(), calls=%async_computation.13 | async-start | bytes 2359296
  461.8 318.4 %reduce-scatter.9.cloned.1.call-start = ((), (), s32[]{:S(2)}) async-start(), calls=%async_computation.10 | async-start | bytes 17301504 | tf_op jit(solution)/shard_map/reduce_scatter | solution.py:254
  514.5 70.9 %copy-start.2 = (bf16[1,128,1024]{2,1,0:T(8,128)(2,1)S(1)}, bf16[1,128,1024]{2,1,0:T(8,128)(2,1)}, u32[]{:S(2)}) copy-start(bf16[1,128,1024]{2,1,0:T(8,128)(2,1)} %param.15) | copy-start | bytes 786436
  585.4 2.2 copy-start.1
  593.7 2.3 copy-start.15
  593.7 536.1 %reduce-scatter.11.cloned.1.call-start = ((), (), s32[]{:S(2)}) async-start(), calls=%async_computation.11 | async-start | bytes 33521664 | tf_op jit(solution)/shard_map/reduce_scatter | solution.py:179
  596.0 5.7 copy-start.17
  596.0 5.7 copy-start.19
  (9 other events, 10.5 us)
Sparse Core Ops, SparseCore 0:
  10.9 71.0 all-gather.7
  86.8 45.2 all-gather.9
  134.9 47.6 all-gather.11
  185.3 56.0 all-gather.13
  244.1 87.1 all-gather.15
  334.0 65.2 all-gather.17
  449.0 64.3 reduce-scatter.12
  516.9 67.2 reduce-scatter.14
  593.8 186.3 reduce-scatter.8
  782.3 347.4 reduce-scatter.10
where the time goes:
time: 1150 us; the launch traced here: 1140 us
  waiting for transfers between devices  856 us (74%)
  blocking collectives  95.5 us (8%)
  matrix products  71.5 us (6%)
  local copies, waits for them, and re-layouts  66.9 us (6%)
  other arithmetic  35.1 us (3%)
  between operations  15.1 us (1%)
    reduce_scatter x1, waiting for transfers between devices, body(): lax.psum_scatter(jnp.concatenate([jnp.einsum('td,tf->df', normed_part, gr...  346 us
    unnamed x12, waiting for transfers between devices  120 us
    reduce_scatter x1, waiting for transfers between devices, body(): lax.psum_scatter(jnp.concatenate([jnp.einsum('td,et->de', normed_part, gr...  103 us
    all_gather x1, waiting for transfers between devices, body(): lax.all_gather(w_in, ('ctx', 'fsdp'), axis=0, tiled=True)  87.4 us
    unnamed x2, blocking collectives  84.1 us
    all_gather x1, waiting for transfers between devices, body(): lax.all_gather(w_out_mlp, ('ctx', 'fsdp'), axis=1, tiled=True)  60.8 us
    all_gather x1, waiting for transfers between devices, body(): lax.all_gather(key_cols.reshape(width, tok_count), 'ctx', axis=1, tiled=T...  41.3 us
    unnamed x48, local copies, waits for them, and re-layouts  37.6 us
  transfers between devices with their start and end apart: 10, of which 10 were waited for; matrix products, arithmetic and copies ran while one was open for 9% of the time, Pallas kernels for 0%

commit v1 on v0

v1 whole, which is shorter than its diff:
```python
import math

import jax
import jax.numpy as jnp
from jax import lax
from jax.experimental import pallas as pl
from jax.experimental.pallas import tpu as pltpu
from jax.sharding import PartitionSpec as P

HEADS = 16
HD = 64


EPSILON = 1e-05
ROPE_BASE = 160000.0
MASKED = -1e30


def layer_norm(values):
    center = values - jnp.mean(values, axis=-1, keepdims=True)
    scaled = lax.rsqrt(jnp.mean(center * center, axis=-1, keepdims=True) + EPSILON)
    return (center * scaled, scaled)


def norm_back(grad_norm, normed, scaled):
    return scaled * (
        grad_norm
        - jnp.mean(grad_norm, axis=-1, keepdims=True)
        - normed * jnp.mean(grad_norm * normed, axis=-1, keepdims=True)
    )


def rope_columns(positions, head_size):
    freqs = ROPE_BASE ** (-jnp.arange(0, head_size, 2, dtype=jnp.float32) / head_size)
    angles = freqs[:, None] * positions[None, :]
    cosine = jnp.concatenate([jnp.cos(angles), jnp.cos(angles)], axis=0)
    sine = jnp.concatenate([jnp.sin(angles), jnp.sin(angles)], axis=0)
    return (cosine[None], sine[None])


def rotate_cols(values, cosine, sine):
    half = values.shape[1] // 2
    turned = jnp.concatenate([-values[:, half:], values[:, :half]], axis=1)
    return values * cosine + turned * sine


def unrotate_cols(grads, cosine, sine):
    half = grads.shape[1] // 2
    weighted = grads * sine
    turned = jnp.concatenate([weighted[:, half:], -weighted[:, :half]], axis=1)
    return grads * cosine + turned


def gelu_slope(values):
    return (
        0.5 * (1.0 + lax.erf(values * 0.7071067811865476))
        + values * jnp.exp(-0.5 * values * values) * 0.3989422804014327
    )


LANES = 128


def masked_scores(query, key, same, scale):
    scores = lax.dot_general(query, key, (((0,), (0,)), ((), ())), preferred_element_type=jnp.float32)
    return jnp.where(same, scores * scale, MASKED)


def same_segment(seg_own_ref, seg_ref, block):
    return seg_own_ref[...] == seg_ref[block, :, :]


def attend_kernel(scale, blocks, query_ref, key_ref, value_ref, seg_own_ref, seg_ref, out_ref, log_ref):
    query = query_ref[0]
    scores = [
        masked_scores(query, key_ref[b, 0, 0], same_segment(seg_own_ref, seg_ref, b), scale)
        for b in range(blocks)
    ]
    peak = scores[0]
    for b in range(1, blocks):
        peak = jnp.maximum(peak, scores[b])
    peak = jnp.max(peak, axis=-1, keepdims=True)
    total = jnp.exp(scores[0] - peak)
    for b in range(1, blocks):
        total = total + jnp.exp(scores[b] - peak)
    log_total = peak + jnp.log(jnp.sum(total, axis=-1, keepdims=True))
    log_ref[0] = log_total
    acc = None
    for b in range(blocks):
        probs = jnp.exp(scores[b] - log_total).astype(jnp.bfloat16)
        term = lax.dot_general(
            value_ref[b, 0, 0], probs, (((1,), (1,)), ((), ())), preferred_element_type=jnp.float32
        )
        acc = term if acc is None else acc + term
    out_ref[0] = acc.astype(jnp.bfloat16)


def attend_grad_kernel(
    scale,
    blocks,
    query_ref,
    key_ref,
    value_ref,
    seg_own_ref,
    seg_ref,
    log_ref,
    grad_ref,
    attended_ref,
    query_grad_ref,
    pair_ref,
):
    query = query_ref[0]
    grad = grad_ref[0]
    log_total = log_ref[0]
    dots_row = jnp.sum(
        grad.astype(jnp.float32) * attended_ref[0].astype(jnp.float32), axis=0, keepdims=True
    )
    dots = jnp.transpose(jnp.broadcast_to(dots_row, (8, dots_row.shape[1])))[:, :1]
    acc = None
    for b in range(blocks):
        key = key_ref[b, 0, 0]
        value = value_ref[b, 0, 0]
        scores = masked_scores(query, key, same_segment(seg_own_ref, seg_ref, b), scale)
        probs = jnp.exp(scores - log_total)
        grad_probs = lax.dot_general(
            grad, value, (((0,), (0,)), ((), ())), preferred_element_type=jnp.float32
        )
        grad_scores = (probs * (grad_probs - dots)).astype(jnp.bfloat16)
        term = lax.dot_general(
            key, grad_scores, (((1,), (1,)), ((), ())), preferred_element_type=jnp.float32
        )
        acc = term if acc is None else acc + term
        key_grad = lax.dot_general(
            query, grad_scores, (((1,), (0,)), ((), ())), preferred_element_type=jnp.float32
        )
        value_grad = lax.dot_general(
            grad,
            probs.astype(jnp.bfloat16),
            (((1,), (0,)), ((), ())),
            preferred_element_type=jnp.float32,
        )
        pair_ref[b, 0, 0] = (key_grad * scale).astype(jnp.bfloat16)
        pair_ref[b, 1, 0] = value_grad.astype(jnp.bfloat16)
    query_grad_ref[0] = acc * scale


def attention_specs(blocks, head_size, tok_count):
    head = pl.BlockSpec((1, head_size, tok_count), lambda h: (h, 0, 0))
    keys = pl.BlockSpec((blocks, 1, 1, head_size, tok_count), lambda h: (0, 0, h, 0, 0))
    values = pl.BlockSpec((blocks, 1, 1, head_size, tok_count), lambda h: (0, 1, h, 0, 0))
    pairs = pl.BlockSpec((blocks, 2, 1, head_size, tok_count), lambda h: (0, 0, h, 0, 0))
    seg_own = pl.BlockSpec((tok_count, 1), lambda h: (0, 0))
    seg_all = pl.BlockSpec((blocks, 1, tok_count), lambda h: (0, 0, 0))
    log = pl.BlockSpec((1, tok_count, 1), lambda h: (h, 0, 0))
    return head, keys, values, pairs, seg_own, seg_all, log


def attend(query_cols, pairs_all, seg_own, seg_all, scale):
    heads, head_size, tok_count = query_cols.shape
    blocks = pairs_all.shape[0]
    head, keys, values, pairs, own, every, log = attention_specs(blocks, head_size, tok_count)
    return pl.pallas_call(
        lambda *refs: attend_kernel(scale, blocks, *refs),
        grid=(heads,),
        in_specs=[head, keys, values, own, every],
        out_specs=[head, log],
        out_shape=[
            jax.ShapeDtypeStruct((heads, head_size, tok_count), jnp.bfloat16),
            jax.ShapeDtypeStruct((heads, tok_count, 1), jnp.float32),
        ],
        name="attend",
    )(query_cols, pairs_all, pairs_all, seg_own, seg_all)


def attend_grads(query_cols, pairs_all, seg_own, seg_all, log_total, grad_cols, attended_cols, scale):
    heads, head_size, tok_count = query_cols.shape
    blocks = pairs_all.shape[0]
    head, keys, values, pairs, own, every, log = attention_specs(blocks, head_size, tok_count)
    return pl.pallas_call(
        lambda *refs: attend_grad_kernel(scale, blocks, *refs),
        grid=(heads,),
        in_specs=[head, keys, values, own, every, log, head, head],
        out_specs=[head, pairs],
        out_shape=[
            jax.ShapeDtypeStruct((heads, head_size, tok_count), jnp.float32),
            jax.ShapeDtypeStruct((blocks, 2, heads, head_size, tok_count), jnp.bfloat16),
        ],
        name="attend_grads",
    )(query_cols, pairs_all, pairs_all, seg_own, seg_all, log_total, grad_cols, attended_cols)


def body(inputs, segment_ids, gain_attn, w_qkv, w_out_attn, gain_mlp, w_in, w_out_mlp, cotangent):
    tokens = inputs[0].astype(jnp.float32)
    tok_count, width = tokens.shape
    heads = HEADS
    head_size = HD
    scale = 1.0 / math.sqrt(head_size)
    everyone = ("ctx", "fsdp")
    hidden_units = w_out_mlp.shape[0]
    gains_own = jnp.concatenate(
        [
            gain_attn[:, None],
            gain_mlp[:, None],
            jnp.zeros((gain_attn.shape[0], LANES - 2), jnp.bfloat16),
        ],
        axis=1,
    )
    first_full = lax.all_gather(
        jnp.concatenate([w_qkv, gains_own], axis=1), everyone, axis=0, tiled=True
    )
    rest_own = jnp.concatenate([w_out_attn, w_in, w_out_mlp.T], axis=1)
    qkv_full = first_full[:, : 3 * width]
    gains = first_full[:, 3 * width : 3 * width + 2].astype(jnp.float32).T
    gain_first = gains[0]
    gain_second = gains[1]
    normed_one, scale_one = layer_norm(tokens)
    normed_attn = (normed_one * gain_first).astype(jnp.bfloat16)
    projected_cols = jnp.einsum(
        "de,td->et", qkv_full, normed_attn, preferred_element_type=jnp.float32
    )
    positions = (lax.axis_index("ctx") * tok_count + jnp.arange(tok_count, dtype=jnp.int32)).astype(
        jnp.float32
    )
    cosine, sine = rope_columns(positions, head_size)
    query_cols = rotate_cols(
        projected_cols[:width].reshape(heads, head_size, tok_count), cosine, sine
    ).astype(jnp.bfloat16)
    key_cols = rotate_cols(
        projected_cols[width : 2 * width].reshape(heads, head_size, tok_count), cosine, sine
    ).astype(jnp.bfloat16)
    value_cols = projected_cols[2 * width :].astype(jnp.bfloat16)
    seg_row = segment_ids.astype(jnp.bfloat16)
    packed = lax.all_gather(
        jnp.concatenate(
            [
                key_cols.reshape(width, tok_count),
                value_cols,
                jnp.broadcast_to(seg_row, (16, tok_count)),
            ],
            axis=0,
        ),
        "ctx",
        axis=0,
        tiled=True,
    )
    blocks = packed.shape[0] // (2 * width + 16)
    packed = packed.reshape(blocks, 2 * width + 16, tok_count)
    rest_full = lax.all_gather(rest_own, everyone, axis=0, tiled=True)
    attn_full = rest_full[:, :width]
    in_full = rest_full[:, width : width + 2 * hidden_units]
    mlp_turned = rest_full[:, width + 2 * hidden_units :]
    pairs_all = packed[:, : 2 * width].reshape(blocks, 2, heads, head_size, tok_count)
    seg_all = packed[:, 2 * width : 2 * width + 1].astype(jnp.float32)
    seg_own = segment_ids.astype(jnp.float32).T
    attended_cols, log_total = attend(query_cols, pairs_all, seg_own, seg_all, scale)
    attended = attended_cols.reshape(width, tok_count).T
    residual = tokens + jnp.dot(attended, attn_full, preferred_element_type=jnp.float32)
    normed_two, scale_two = layer_norm(residual)
    normed_mlp = (normed_two * gain_second).astype(jnp.bfloat16)
    expanded = jnp.dot(normed_mlp, in_full, preferred_element_type=jnp.float32)
    pre_act = expanded[:, :hidden_units]
    gate_part = expanded[:, hidden_units:]
    activated = jax.nn.gelu(pre_act, approximate=False)
    product = (activated * gate_part).astype(jnp.bfloat16)
    block_out = (
        residual
        + jnp.einsum("tf,df->td", product, mlp_turned, preferred_element_type=jnp.float32)
    ).astype(jnp.bfloat16)
    grad_out = cotangent[0]
    grad_product = jnp.einsum("td,df->tf", grad_out, mlp_turned, preferred_element_type=jnp.float32)
    grad_expanded = jnp.concatenate(
        [grad_product * gate_part * gelu_slope(pre_act), grad_product * activated], axis=1
    ).astype(jnp.bfloat16)
    grad_normed_mlp = jnp.einsum(
        "tf,df->td", grad_expanded, in_full, preferred_element_type=jnp.float32
    )
    grad_gain_two = jnp.sum(grad_normed_mlp * normed_two, axis=0)
    mlp_rows = lax.psum_scatter(
        jnp.concatenate(
            [
                jnp.einsum(
                    "td,tf->df", normed_mlp, grad_expanded, preferred_element_type=jnp.float32
                ).astype(jnp.bfloat16),
                jnp.einsum(
                    "td,tf->df", grad_out, product, preferred_element_type=jnp.float32
                ).astype(jnp.bfloat16),
            ],
            axis=1,
        ),
        everyone,
        scatter_dimension=0,
        tiled=True,
    )
    grad_residual = grad_out.astype(jnp.float32) + norm_back(
        grad_normed_mlp * gain_second, normed_two, scale_two
    )
    residual_half = grad_residual.astype(jnp.bfloat16)
    grad_attended = jnp.einsum(
        "te,de->dt", residual_half, attn_full, preferred_element_type=jnp.float32
    ).astype(jnp.bfloat16)
    grad_att_cols = grad_attended.reshape(heads, head_size, tok_count)
    grad_query_cols, pair_parts = attend_grads(
        query_cols, pairs_all, seg_own, seg_all, log_total, grad_att_cols, attended_cols, scale
    )
    pair_sums = lax.psum_scatter(
        pair_parts.reshape(blocks * 2 * width, tok_count), "ctx", scatter_dimension=0, tiled=True
    )
    grad_keys = pair_sums[:width].astype(jnp.float32)
    grad_values = pair_sums[width:]
    grad_key_cols = grad_keys.reshape(heads, head_size, tok_count)
    grad_query_rot = unrotate_cols(grad_query_cols, cosine, sine).reshape(width, tok_count)
    grad_key_rot = unrotate_cols(grad_key_cols, cosine, sine).reshape(width, tok_count)
    grad_proj_cols = jnp.concatenate(
        [grad_query_rot.astype(jnp.bfloat16), grad_key_rot.astype(jnp.bfloat16), grad_values], axis=0
    )
    grad_normed_attn = jnp.einsum(
        "de,et->td", qkv_full, grad_proj_cols, preferred_element_type=jnp.float32
    )
    grad_gain_one = jnp.sum(grad_normed_attn * normed_one, axis=0)
    gain_cols = jnp.concatenate(
        [
            jnp.stack([grad_gain_one, grad_gain_two], axis=0),
            jnp.zeros((LANES - 2, width), jnp.float32),
        ],
        axis=0,
    ).T.astype(jnp.bfloat16)
    attn_rows = lax.psum_scatter(
        jnp.concatenate(
            [
                jnp.einsum(
                    "td,et->de", normed_attn, grad_proj_cols, preferred_element_type=jnp.float32
                ).astype(jnp.bfloat16),
                jnp.einsum(
                    "td,te->de", attended, residual_half, preferred_element_type=jnp.float32
                ).astype(jnp.bfloat16),
                gain_cols,
            ],
            axis=1,
        ),
        everyone,
        scatter_dimension=0,
        tiled=True,
    )
    grad_tokens = (
        grad_residual + norm_back(grad_normed_attn * gain_first, normed_one, scale_one)
    ).astype(jnp.bfloat16)
    attn_sums = attn_rows.astype(jnp.float32)
    mlp_sums = mlp_rows.astype(jnp.float32)
    grad_qkv_rows = attn_sums[:, : 3 * width]
    grad_attn_rows = attn_sums[:, 3 * width : 4 * width]
    gain_sum_one = attn_sums[:, 4 * width]
    gain_sum_two = attn_sums[:, 4 * width + 1]
    grad_in_rows = mlp_sums[:, : 2 * hidden_units]
    grad_mlp_cols = mlp_sums[:, 2 * hidden_units :].T
    return (
        block_out[None],
        grad_tokens[None],
        grad_qkv_rows,
        grad_attn_rows,
        grad_in_rows,
        grad_mlp_cols,
        gain_sum_one,
        gain_sum_two,
    )


def solution(mesh):
    in_specs = (
        P("fsdp", "ctx", None),
        P("fsdp", "ctx"),
        P(("ctx", "fsdp")),
        P(("ctx", "fsdp"), None),
        P(("ctx", "fsdp"), None),
        P(("ctx", "fsdp")),
        P(("ctx", "fsdp"), None),
        P(None, ("ctx", "fsdp")),
        P("fsdp", "ctx", None),
    )
    out_specs = (
        P("fsdp", "ctx", None),
        P("fsdp", "ctx", None),
        P(("ctx", "fsdp"), None),
        P(("ctx", "fsdp"), None),
        P(("ctx", "fsdp"), None),
        P(None, ("ctx", "fsdp")),
        P(("ctx", "fsdp")),
        P(("ctx", "fsdp")),
    )
    return jax.shard_map(body, mesh=mesh, in_specs=in_specs, out_specs=out_specs, check_vma=False)
```

time: 1150 us -> 766 us (0.67)
  waiting for transfers between devices: 856 us -> 600 us
  blocking collectives: 95.5 us -> 0 us
  Pallas kernels: 0 us -> 44.1 us
  local copies, waits for them, and re-layouts: 66.9 us -> 27.3 us
  matrix products: 71.5 us -> 51.4 us
    unnamed x12 -> x6, waiting for transfers between devices: 120 us -> 0.1 us
    reduce_scatter x2 -> x3, waiting for transfers between devices: 450 us -> 360 us  [the longest x1 177 us: body(): lax.psum_scatter(jnp.concatenate([jnp.einsum('td,tf->df', normed_mlp, gra...]
    unnamed x2 -> x0, blocking collectives: 84.1 us -> none
    all_gather x6 -> x3, waiting for transfers between devices: 286 us -> 240 us  [the longest x1 105 us: body(): rest_full = lax.all_gather(rest_own, everyone, axis=0, tiled=True)]
    pallas_call x0 -> x2, Pallas kernels: none -> 44.1 us  [the longest x1 28.4 us: attend_grads(): pl.pallas_call(lambda *refs: attend_grad_kernel(scale, blocks, *refs), gr...]
    unnamed x48 -> x56, local copies, waits for them, and re-layouts: 37.6 us -> 3.15 us
    dot_general x18 -> x4, matrix products: 39.4 us -> 19.3 us  [the longest x1 8.3 us: body(): jnp.einsum('td,df->tf', grad_out, mlp_turned, preferred_element_type=jnp....]
  transfers between devices with their start and end apart: 10 -> 6, of which waited for: 10 -> 6; matrix products, arithmetic and copies ran while one was open for 9% -> 7% of each run, Pallas kernels for 0% -> 2%
where the time goes in v1:
time: 766 us; the launch traced here: 763 us
  waiting for transfers between devices  600 us (78%)
  matrix products  51.4 us (7%)
  Pallas kernels  44.1 us (6%)
  local copies, waits for them, and re-layouts  27.3 us (4%)
  other arithmetic  25.6 us (3%)
  between operations  14.6 us (2%)
    reduce_scatter x1, waiting for transfers between devices, body(): lax.psum_scatter(jnp.concatenate([jnp.einsum('td,tf->df', normed_mlp, gra...  177 us
    all_gather x1, waiting for transfers between devices, body(): rest_full = lax.all_gather(rest_own, everyone, axis=0, tiled=True)  105 us
    reduce_scatter x1, waiting for transfers between devices, body(): lax.psum_scatter(jnp.concatenate([jnp.einsum('td,et->de', normed_attn, gr...  98.3 us
    reduce_scatter x1, waiting for transfers between devices, body(): lax.psum_scatter(pair_parts.reshape(blocks * 2 * width, tok_count), 'ctx'...  84.3 us
    all_gather x1, waiting for transfers between devices, body(): lax.all_gather(jnp.concatenate([w_qkv, gains_own], axis=1), everyone, axi...  69.5 us
    all_gather x1, waiting for transfers between devices, body(): lax.all_gather(jnp.concatenate([key_cols.reshape(width, tok_count), value...  65.7 us
    pallas_call x1, Pallas kernels, attend_grads(): pl.pallas_call(lambda *refs: attend_grad_kernel(scale, blocks, *refs), gr...  28.4 us
    pallas_call x1, Pallas kernels, attend(): pl.pallas_call(lambda *refs: attend_kernel(scale, blocks, *refs), grid=(h...  15.7 us
  transfers between devices with their start and end apart: 6, of which 6 were waited for; matrix products, arithmetic and copies ran while one was open for 7% of the time, Pallas kernels for 2%

profile of v1, /device:TPU:11, one launch (start us, length us, event | category | flops | bytes accessed | tf_op | source)
XLA Modules:
  0.0 763.2 jit_solution(14789423281492682601)
XLA Ops:
  8.7 1.7 concatenate.46
  11.8 1.2 fusion.64
  13.7 69.5 %all-gather.4.cloned.1.call-done = bf16[1024,3200]{1,0:T(8,128)(2,1)} async-done(((bf16[32,3200]{1,0:T(8,128)(2,1)}), bf16[1024,3200]{1,0:T(8,128)(2,1)}) %all-gather.4.cloned.1.call-update) | async-done | bytes 6553616 | tf_op jit(solution)/shard_map/all_gather | solution.py:208
  84.7 4.7 fusion.6
  93.5 65.7 %all-gather.6.cloned.1.call-done = bf16[16512,128]{1,0:T(8,128)(2,1)} async-done(((bf16[2064,128]{1,0:T(8,128)(2,1)}), bf16[16512,128]{1,0:T(8,128)(2,1)}) %all-gather.6.cloned.1.call-update) | async-done | bytes 4227088 | tf_op jit(solution)/shard_map/all_gather | solution.py:233
  159.3 4.4 slice.131
  163.7 1.3 slice_convert_fusion.2.refs_4_
  165.0 15.7 %attend.1 = (bf16[16,64,128]{2,1,0:T(8,128)(2,1)}, f32[16,128,1]{2,1,0:T(8,128)}) custom-call(bf16[16,64,128]{2,1,0:T(8,128)(2,1)} %fusion.70.refs_0_, bf16[8,2,16,64,128]{4,3,2,1,0:T(8,128)(2,1)} %bitcast.95, bf16[8,2,16,64,128]{4,3,2,1,0:T(8,128)(2,1)} %bitcast.96, f32[128,1]{1,0:T(8,128)} %copy.35.refs_3_, f32[8,1,128]{2,1,0:T(1,128)} %slice_convert_fusion.2.refs_4_), custom_call_target="tpu_custom_call" | custom-call | tf_op jit(solution)/shard_map/attend/pallas_call | solution.py:162
  180.7 104.5 %all-gather.8.cloned.1.call-done = bf16[1024,8896]{1,0:T(8,128)(2,1)} async-done(((bf16[32,8896]{1,0:T(8,128)(2,1)}), bf16[1024,8896]{1,0:T(8,128)(2,1)}) %all-gather.8.cloned.1.call-update) | async-done | bytes 18219024 | tf_op jit(solution)/shard_map/all_gather | solution.py:248
  285.2 2.2 fusion.86
  287.7 5.8 fusion.2
  293.5 8.3 %multiply_convert_fusion = (bf16[128,2624]{1,0:T(8,128)(2,1)S(1)}, f32[128,2624]{1,0:T(8,128)}, bf16[128,2624]{1,0:T(8,128)(2,1)S(1)}) fusion(f32[128,5248]{1,0:T(8,128)S(1)} %fusion.2, bf16[1024,8896]{1,0:T(8,128)(2,1)} %all-gather.8.cloned.1.call-done, bf16[1,128,1024]{2,1,0:T(8,128)(2,1)S(1)} %copy-done.9), kind=kOutput, calls=%fused_computation.34 | convolution fusion | flops 713728000 | bytes 11141120 | tf_op jit(solution)/shard_map/td,df->tf/dot_general | solution.py:270
  301.8 7.0 multiply_reduce_fusion
  309.1 3.2 fusion.44
  312.3 28.4 %attend_grads.1 = (f32[16,64,128]{2,1,0:T(8,128)}, bf16[8,2,16,64,128]{4,3,2,1,0:T(8,128)(2,1)}) custom-call(bf16[16,64,128]{2,1,0:T(8,128)(2,1)} %fusion.70.refs_0_, bf16[8,2,16,64,128]{4,3,2,1,0:T(8,128)(2,1)} %bitcast.97, bf16[8,2,16,64,128]{4,3,2,1,0:T(8,128)(2,1)} %bitcast.98, f32[128,1]{1,0:T(8,128)} %copy.35.refs_3_, ...), custom_call_target="tpu_custom_call" | custom-call | tf_op jit(solution)/shard_map/attend_grads/pallas_call | solution.py:179
  342.1 1.7 convolution_convert_fusion.3
  343.8 84.3 %reduce-scatter.4.cloned.1.call-done = bf16[2048,128]{1,0:T(8,128)(2,1)} async-done(((bf16[16384,128]{1,0:T(8,128)(2,1)}), bf16[2048,128]{1,0:T(8,128)(2,1)}) %reduce-scatter.4.cloned.1.call-update) | async-done | bytes 524304 | tf_op jit(solution)/shard_map/reduce_scatter | solution.py:305
  430.6 2.0 convolution_convert_fusion.2
  433.2 3.5 fusion.63
  437.1 3.8 pad_maximum_fusion.1
  441.0 1.3 copy-done.7
  442.2 1.8 multiply_convert_fusion.1
  444.0 3.9 fusion.8
  447.9 8.5 %copy.41 = bf16[1024,2624]{1,0:T(8,128)(2,1)} copy(bf16[1024,2624]{0,1:T(8,128)(2,1)} %fusion.8) | data formatting | bytes 10747904 | tf_op jit(solution)/shard_map/convert_element_type | solution.py:286
  456.4 3.5 convolution_convert_fusion
  459.9 6.6 pad_maximum_fusion
  466.6 5.5 fusion.47
  473.1 98.3 %reduce-scatter.6.cloned.1.call-done = bf16[32,4224]{1,0:T(8,128)(2,1)} async-done(((bf16[1024,4224]{1,0:T(8,128)(2,1)}), bf16[32,4224]{1,0:T(8,128)(2,1)}) %reduce-scatter.6.cloned.1.call-update) | async-done | bytes 270352 | tf_op jit(solution)/shard_map/reduce_scatter | solution.py:327
  571.4 1.7 slice.145
  573.1 1.5 slice.146
  576.3 177.2 %reduce-scatter.8.cloned.1.call-done = bf16[32,7872]{1,0:T(8,128)(2,1)} async-done(((bf16[1024,7872]{1,0:T(8,128)(2,1)}), bf16[32,7872]{1,0:T(8,128)(2,1)}) %reduce-scatter.8.cloned.1.call-update) | async-done | bytes 503824 | tf_op jit(solution)/shard_map/reduce_scatter | solution.py:278
  753.5 1.2 convert_element_type.120
  (117 shorter events, 18.8 us)
Async XLA Ops:
  7.2 76.0 %all-gather.4.cloned.1.call-start = ((), (), s32[]{:S(2)}) async-start(), calls=%async_computation.3 | async-start | bytes 6758400 | tf_op jit(solution)/shard_map/all_gather | solution.py:208
  10.4 74.2 %copy-start.1 = (bf16[1,128,1024]{2,1,0:T(8,128)(2,1)S(1)}, bf16[1,128,1024]{2,1,0:T(8,128)(2,1)}, u32[]{:S(2)}) copy-start(bf16[1,128,1024]{2,1,0:T(8,128)(2,1)} %param.9) | copy-start | bytes 786436
  10.4 148.8 %all-gather.6.cloned.1.call-start = ((), (), s32[]{:S(2)}) async-start(), calls=%async_computation.4 | async-start | bytes 4755456 | tf_op jit(solution)/shard_map/all_gather | solution.py:233
  10.7 82.1 %copy-start.11 = (f32[64,128]{1,0:T(8,128)}, f32[64,128]{1,0:T(8,128)S(1)}, u32[]{:S(2)}) copy-start(f32[64,128]{1,0:T(8,128)S(1)} %get-tuple-element.51) | copy-start | bytes 98308
  10.7 82.1 %copy-start.18 = (f32[64,128]{1,0:T(8,128)}, f32[64,128]{1,0:T(8,128)S(1)}, u32[]{:S(2)}) copy-start(f32[64,128]{1,0:T(8,128)S(1)} %get-tuple-element.52) | copy-start | bytes 98308
  89.6 1.2 copy-start.22
  89.7 1.2 copy-start.23
  90.6 194.6 %all-gather.8.cloned.1.call-start = ((), (), s32[]{:S(2)}) async-start(), calls=%async_computation.5 | async-start | bytes 18923520 | tf_op jit(solution)/shard_map/all_gather | solution.py:248
  91.7 336.4 %reduce-scatter.4.cloned.1.call-start = ((), (), s32[]{:S(2)}) async-start(), calls=%async_computation.6 | async-start | bytes 4718592 | tf_op jit(solution)/shard_map/reduce_scatter | solution.py:305
  287.6 5.8 copy-start.9
  293.4 8.3 %copy-start.13 = (f32[128,5248]{1,0:T(8,128)}, f32[128,5248]{1,0:T(8,128)S(1)}, u32[]{:S(2)}) copy-start(f32[128,5248]{1,0:T(8,128)S(1)} %fusion.2) | copy-start | bytes 8060932
  301.8 7.0 copy-start.14
  301.8 7.0 copy-start.16
  309.1 31.7 %copy-start.2 = (f32[128,1024]{1,0:T(8,128)}, f32[128,1024]{1,0:T(8,128)S(1)}, u32[]{:S(2)}) copy-start(f32[128,1024]{1,0:T(8,128)S(1)} %multiply_add_fusion) | copy-start | bytes 1572868
  340.8 1.3 copy-start.5
  340.8 230.6 %reduce-scatter.6.cloned.1.call-start = ((), (), s32[]{:S(2)}) async-start(), calls=%async_computation.7 | async-start | bytes 8921088 | tf_op jit(solution)/shard_map/reduce_scatter | solution.py:327
  342.1 87.2 %copy-start.19 = (f32[64,128]{1,0:T(8,128)S(1)}, f32[64,128]{1,0:T(8,128)}, u32[]{:S(2)}) copy-start(f32[64,128]{1,0:T(8,128)} %copy-done.18) | copy-start | bytes 98308
  428.1 1.2 copy-start.6
  429.5 1.0 copy-start.8
  430.1 2.4 slice-start
  430.6 2.6 slice-start.1
  433.2 3.7 copy-start.10
  440.9 1.3 copy-start.7
  440.9 312.6 %reduce-scatter.8.cloned.1.call-start = ((), (), s32[]{:S(2)}) async-start(), calls=%async_computation.8 | async-start | bytes 16760832 | tf_op jit(solution)/shard_map/reduce_scatter | solution.py:278
  447.9 8.5 %copy-start.15 = (bf16[128,2624]{1,0:T(8,128)(2,1)S(1)}, bf16[128,2624]{1,0:T(8,128)(2,1)}, u32[]{:S(2)}) copy-start(bf16[128,2624]{1,0:T(8,128)(2,1)} %copy-done.14) | copy-start | bytes 2015236
  447.9 8.5 %copy-start.17 = (bf16[128,2624]{1,0:T(8,128)(2,1)S(1)}, bf16[128,2624]{1,0:T(8,128)(2,1)}, u32[]{:S(2)}) copy-start(bf16[128,2624]{1,0:T(8,128)(2,1)} %copy-done.16) | copy-start | bytes 2015236
  456.4 3.5 copy-start
  466.6 5.6 copy-start.25
  466.6 5.6 copy-start.24
  466.6 5.6 copy-start.3
  466.6 5.6 copy-start.20
  753.5 1.9 copy-start.4
  (2 other events, 1.8 us)
Sparse Core Ops, SparseCore 0:
  11.4 71.6 all-gather.3
  90.7 68.5 all-gather.5
  162.7 122.4 all-gather.7
  340.9 87.1 reduce-scatter.3
  441.0 130.3 reduce-scatter.5
  573.6 179.8 reduce-scatter.7

commit v2 on v1

v2 whole, which is shorter than its diff:
```python
import functools
import math

import jax
import jax.numpy as jnp
from jax import lax
from jax.experimental import pallas as pl
from jax.experimental.pallas import tpu as pltpu
from jax.sharding import PartitionSpec as P

HEADS = 16
HD = 64


EPSILON = 1e-05
ROPE_BASE = 160000.0
MASKED = -1e30


def layer_norm(values):
    center = values - jnp.mean(values, axis=-1, keepdims=True)
    scaled = lax.rsqrt(jnp.mean(center * center, axis=-1, keepdims=True) + EPSILON)
    return (center * scaled, scaled)


def norm_back(grad_norm, normed, scaled):
    return scaled * (
        grad_norm
        - jnp.mean(grad_norm, axis=-1, keepdims=True)
        - normed * jnp.mean(grad_norm * normed, axis=-1, keepdims=True)
    )


def rope_columns(positions, head_size):
    freqs = ROPE_BASE ** (-jnp.arange(0, head_size, 2, dtype=jnp.float32) / head_size)
    angles = freqs[:, None] * positions[None, :]
    cosine = jnp.concatenate([jnp.cos(angles), jnp.cos(angles)], axis=0)
    sine = jnp.concatenate([jnp.sin(angles), jnp.sin(angles)], axis=0)
    return (cosine[None], sine[None])


def rotate_cols(values, cosine, sine):
    half = values.shape[1] // 2
    turned = jnp.concatenate([-values[:, half:], values[:, :half]], axis=1)
    return values * cosine + turned * sine


def unrotate_cols(grads, cosine, sine):
    half = grads.shape[1] // 2
    weighted = grads * sine
    turned = jnp.concatenate([weighted[:, half:], -weighted[:, :half]], axis=1)
    return grads * cosine + turned


def gelu_slope(values):
    return (
        0.5 * (1.0 + lax.erf(values * 0.7071067811865476))
        + values * jnp.exp(-0.5 * values * values) * 0.3989422804014327
    )


LANES = 128
SEG_ROWS = 16
QUERY_BLOCK = 256


def masked_scores(query, key, same, scale):
    scores = lax.dot_general(query, key, (((0,), (0,)), ((), ())), preferred_element_type=jnp.float32)
    return jnp.where(same, scores * scale, MASKED)


def attend_kernel(scale, query_ref, key_ref, value_ref, seg_own_ref, seg_ref, out_ref, log_ref):
    same = seg_own_ref[...] == seg_ref[...]
    scores = masked_scores(query_ref[0], key_ref[0], same, scale)
    peak = jnp.max(scores, axis=-1, keepdims=True)
    log_total = peak + jnp.log(jnp.sum(jnp.exp(scores - peak), axis=-1, keepdims=True))
    log_ref[0] = log_total
    probs = jnp.exp(scores - log_total).astype(jnp.bfloat16)
    out_ref[0] = lax.dot_general(
        value_ref[0], probs, (((1,), (1,)), ((), ())), preferred_element_type=jnp.float32
    ).astype(jnp.bfloat16)


def attend_grad_kernel(
    scale,
    query_ref,
    key_ref,
    value_ref,
    seg_own_ref,
    seg_ref,
    log_ref,
    grad_ref,
    attended_ref,
    query_grad_ref,
    key_grad_ref,
    value_grad_ref,
):
    @pl.when(pl.program_id(1) == 0)
    def _():
        key_grad_ref[...] = jnp.zeros_like(key_grad_ref)
        value_grad_ref[...] = jnp.zeros_like(value_grad_ref)

    query = query_ref[0]
    grad = grad_ref[0]
    key = key_ref[0]
    dots_row = jnp.sum(
        grad.astype(jnp.float32) * attended_ref[0].astype(jnp.float32), axis=0, keepdims=True
    )
    dots = jnp.transpose(jnp.broadcast_to(dots_row, (8, dots_row.shape[1])))[:, :1]
    same = seg_own_ref[...] == seg_ref[...]
    probs = jnp.exp(masked_scores(query, key, same, scale) - log_ref[0])
    grad_probs = lax.dot_general(
        grad, value_ref[0], (((0,), (0,)), ((), ())), preferred_element_type=jnp.float32
    )
    grad_scores = (probs * (grad_probs - dots)).astype(jnp.bfloat16)
    query_grad_ref[0] = scale * lax.dot_general(
        key, grad_scores, (((1,), (1,)), ((), ())), preferred_element_type=jnp.float32
    )
    key_grad_ref[0] += scale * lax.dot_general(
        query, grad_scores, (((1,), (0,)), ((), ())), preferred_element_type=jnp.float32
    )
    value_grad_ref[0] += lax.dot_general(
        grad, probs.astype(jnp.bfloat16), (((1,), (0,)), ((), ())), preferred_element_type=jnp.float32
    )


def attention_specs(head_size, row_count, block):
    part = pl.BlockSpec((1, head_size, block), lambda h, b: (h, 0, b))
    full = pl.BlockSpec((1, head_size, row_count), lambda h, b: (h, 0, 0))
    seg_own = pl.BlockSpec((block, 1), lambda h, b: (b, 0))
    seg_all = pl.BlockSpec((1, row_count), lambda h, b: (0, 0))
    log = pl.BlockSpec((1, block, 1), lambda h, b: (h, b, 0))
    return part, full, seg_own, seg_all, log


def attend(query_cols, key_cols, value_cols, seg_col, seg_row, scale):
    heads, head_size, row_count = query_cols.shape
    block = min(QUERY_BLOCK, row_count)
    part, full, own, every, log = attention_specs(head_size, row_count, block)
    return pl.pallas_call(
        lambda *refs: attend_kernel(scale, *refs),
        grid=(heads, row_count // block),
        in_specs=[part, full, full, own, every],
        out_specs=[part, log],
        out_shape=[
            jax.ShapeDtypeStruct((heads, head_size, row_count), jnp.bfloat16),
            jax.ShapeDtypeStruct((heads, row_count, 1), jnp.float32),
        ],
        name="attend",
    )(query_cols, key_cols, value_cols, seg_col, seg_row)


def attend_grads(
    query_cols, key_cols, value_cols, seg_col, seg_row, log_total, grad_cols, attended_cols, scale
):
    heads, head_size, row_count = query_cols.shape
    block = min(QUERY_BLOCK, row_count)
    part, full, own, every, log = attention_specs(head_size, row_count, block)
    grads = jax.ShapeDtypeStruct((heads, head_size, row_count), jnp.float32)
    return pl.pallas_call(
        lambda *refs: attend_grad_kernel(scale, *refs),
        grid=(heads, row_count // block),
        in_specs=[part, full, full, own, every, log, part, part],
        out_specs=[part, full, full],
        out_shape=[grads, grads, grads],
        name="attend_grads",
    )(query_cols, key_cols, value_cols, seg_col, seg_row, log_total, grad_cols, attended_cols)


def body(
    ctx_size,
    fsdp_size,
    inputs,
    segment_ids,
    gain_attn,
    w_qkv,
    w_out_attn,
    gain_mlp,
    w_in,
    w_out_mlp,
    cotangent,
):
    tok_count, width = inputs.shape[1:]
    heads = HEADS
    head_size = HD
    scale = 1.0 / math.sqrt(head_size)
    everyone = ("ctx", "fsdp")
    hidden_units = w_out_mlp.shape[0]
    row_count = ctx_size * tok_count
    devices = ctx_size * fsdp_size
    own_heads = heads // ctx_size
    own_width = own_heads * head_size
    weight_rows = w_qkv.shape[0]

    seg_block = jnp.pad(segment_ids.astype(jnp.bfloat16), ((0, SEG_ROWS - 1), (0, width - tok_count)))
    gathered = lax.all_gather(
        jnp.concatenate([inputs[0], seg_block], axis=0), "ctx", axis=0, tiled=True
    ).reshape(ctx_size, tok_count + SEG_ROWS, width)

    qkv_parts = jnp.transpose(
        w_qkv.reshape(weight_rows, 3, ctx_size, own_width), (2, 0, 1, 3)
    ).reshape(ctx_size, weight_rows, 3 * own_width)
    gains_own = jnp.pad(jnp.stack([gain_attn, gain_mlp], axis=1), ((0, 0), (0, LANES - 2)))
    qkv_parts = jnp.concatenate(
        [qkv_parts, jnp.broadcast_to(gains_own, (ctx_size, weight_rows, LANES))], axis=2
    )
    qkv_parts = jnp.broadcast_to(
        qkv_parts[:, None], (ctx_size, fsdp_size, weight_rows, 3 * own_width + LANES)
    ).reshape(devices, weight_rows, 3 * own_width + LANES)
    qkv_got = lax.all_to_all(qkv_parts, everyone, 0, 0, tiled=True).reshape(
        devices * weight_rows, 3 * own_width + LANES
    )
    qkv_mine = qkv_got[:, : 3 * own_width]
    gains = qkv_got[:, 3 * own_width : 3 * own_width + 2].astype(jnp.float32).T
    gain_first = gains[0]
    gain_second = gains[1]

    rest_own = jnp.concatenate([w_out_attn, w_in, w_out_mlp.T], axis=1)
    rest_own, gathered = lax.optimization_barrier((rest_own, gathered))
    rest_full = lax.all_gather(rest_own, everyone, axis=0, tiled=True)
    attn_full = rest_full[:, :width]
    in_full = rest_full[:, width : width + 2 * hidden_units]
    mlp_turned = rest_full[:, width + 2 * hidden_units :]

    seg_row = gathered[:, tok_count, :tok_count].reshape(1, row_count).astype(jnp.float32)
    seg_col = seg_row.reshape(row_count, 1)
    row_tokens = gathered[:, :tok_count].reshape(row_count, width).astype(jnp.float32)
    row_normed, unused = layer_norm(row_tokens)
    row_normed_attn = (row_normed * gain_first).astype(jnp.bfloat16)
    tokens = inputs[0].astype(jnp.float32)
    normed_one, scale_one = layer_norm(tokens)

    projected_cols = jnp.einsum(
        "de,td->et", qkv_mine, row_normed_attn, preferred_element_type=jnp.float32
    ).reshape(3, own_heads, head_size, row_count)
    positions = jnp.arange(row_count, dtype=jnp.int32).astype(jnp.float32)
    cosine, sine = rope_columns(positions, head_size)
    query_cols = rotate_cols(projected_cols[0], cosine, sine).astype(jnp.bfloat16)
    key_cols = rotate_cols(projected_cols[1], cosine, sine).astype(jnp.bfloat16)
    value_cols = projected_cols[2].astype(jnp.bfloat16)
    row_attended, log_total = attend(query_cols, key_cols, value_cols, seg_col, seg_row, scale)

    attended = lax.all_to_all(
        row_attended.reshape(own_width, row_count).T.reshape(ctx_size, tok_count, own_width),
        "ctx",
        0,
        0,
        tiled=True,
    )
    attended = jnp.transpose(attended, (1, 0, 2)).reshape(tok_count, width)
    residual = tokens + jnp.dot(attended, attn_full, preferred_element_type=jnp.float32)
    normed_two, scale_two = layer_norm(residual)
    normed_mlp = (normed_two * gain_second).astype(jnp.bfloat16)
    expanded = jnp.dot(normed_mlp, in_full, preferred_element_type=jnp.float32)
    pre_act = expanded[:, :hidden_units]
    gate_part = expanded[:, hidden_units:]
    activated = jax.nn.gelu(pre_act, approximate=False)
    product = (activated * gate_part).astype(jnp.bfloat16)
    block_out = (
        residual
        + jnp.einsum("tf,df->td", product, mlp_turned, preferred_element_type=jnp.float32)
    ).astype(jnp.bfloat16)
    grad_out = cotangent[0]
    grad_product = jnp.einsum("td,df->tf", grad_out, mlp_turned, preferred_element_type=jnp.float32)
    grad_expanded = jnp.concatenate(
        [grad_product * gate_part * gelu_slope(pre_act), grad_product * activated], axis=1
    ).astype(jnp.bfloat16)
    grad_normed_mlp = jnp.einsum(
        "tf,df->td", grad_expanded, in_full, preferred_element_type=jnp.float32
    )
    grad_gain_two = jnp.sum(grad_normed_mlp * normed_two, axis=0)
    grad_residual = grad_out.astype(jnp.float32) + norm_back(
        grad_normed_mlp * gain_second, normed_two, scale_two
    )
    residual_half = grad_residual.astype(jnp.bfloat16)
    gain_block = jnp.pad(grad_gain_two[:, None], ((0, 0), (0, LANES - 1))).astype(jnp.bfloat16)
    weight_sums = lax.psum_scatter(
        jnp.concatenate(
            [
                jnp.einsum(
                    "td,te->de", attended, residual_half, preferred_element_type=jnp.float32
                ).astype(jnp.bfloat16),
                jnp.einsum(
                    "td,tf->df", normed_mlp, grad_expanded, preferred_element_type=jnp.float32
                ).astype(jnp.bfloat16),
                jnp.einsum(
                    "td,tf->df", grad_out, product, preferred_element_type=jnp.float32
                ).astype(jnp.bfloat16),
                gain_block,
            ],
            axis=1,
        ),
        everyone,
        scatter_dimension=0,
        tiled=True,
    ).astype(jnp.float32)
    grad_attended = jnp.einsum(
        "te,de->td", residual_half, attn_full, preferred_element_type=jnp.float32
    ).astype(jnp.bfloat16)
    row_grad = lax.all_to_all(
        jnp.transpose(grad_attended.reshape(tok_count, ctx_size, own_width), (1, 0, 2)),
        "ctx",
        0,
        0,
        tiled=True,
    )
    row_grad_cols = row_grad.reshape(row_count, own_width).T.reshape(
        own_heads, head_size, row_count
    )
    grad_query, grad_key, grad_value = attend_grads(
        query_cols,
        key_cols,
        value_cols,
        seg_col,
        seg_row,
        log_total,
        row_grad_cols,
        row_attended,
        scale,
    )
    grad_proj_cols = (
        jnp.stack(
            [
                unrotate_cols(grad_query, cosine, sine),
                unrotate_cols(grad_key, cosine, sine),
                grad_value,
            ],
            axis=0,
        )
        .astype(jnp.bfloat16)
        .reshape(3 * own_width, row_count)
    )
    row_grad_normed = jnp.einsum(
        "de,et->td", qkv_mine, grad_proj_cols, preferred_element_type=jnp.float32
    )
    grad_gain_part = jnp.sum(row_grad_normed * row_normed, axis=0)
    grad_normed_attn = jnp.sum(
        lax.all_to_all(
            row_grad_normed.astype(jnp.bfloat16).reshape(ctx_size, tok_count, width),
            "ctx",
            0,
            0,
            tiled=True,
        ).astype(jnp.float32),
        axis=0,
    )
    qkv_terms = jnp.concatenate(
        [
            jnp.einsum(
                "td,et->de", row_normed_attn, grad_proj_cols, preferred_element_type=jnp.float32
            ).astype(jnp.bfloat16),
            jnp.pad(grad_gain_part[:, None], ((0, 0), (0, LANES - 1))).astype(jnp.bfloat16),
        ],
        axis=1,
    ).reshape(devices, weight_rows, 3 * own_width + LANES)
    qkv_sums = jnp.sum(
        lax.all_to_all(qkv_terms, everyone, 0, 0, tiled=True)
        .reshape(ctx_size, fsdp_size, weight_rows, 3 * own_width + LANES)
        .astype(jnp.float32),
        axis=1,
    )
    grad_qkv_rows = jnp.transpose(
        qkv_sums[:, :, : 3 * own_width].reshape(ctx_size, weight_rows, 3, own_width), (1, 2, 0, 3)
    ).reshape(weight_rows, 3 * width)
    gain_sum_one = jnp.sum(qkv_sums[:, :, 3 * own_width], axis=0)
    grad_tokens = (
        grad_residual + norm_back(grad_normed_attn * gain_first, normed_one, scale_one)
    ).astype(jnp.bfloat16)
    grad_attn_rows = weight_sums[:, :width]
    grad_in_rows = weight_sums[:, width : width + 2 * hidden_units]
    grad_mlp_cols = weight_sums[:, width + 2 * hidden_units : width + 3 * hidden_units].T
    gain_sum_two = weight_sums[:, width + 3 * hidden_units]
    return (
        block_out[None],
        grad_tokens[None],
        grad_qkv_rows,
        grad_attn_rows,
        grad_in_rows,
        grad_mlp_cols,
        gain_sum_one,
        gain_sum_two,
    )


def solution(mesh):
    in_specs = (
        P("fsdp", "ctx", None),
        P("fsdp", "ctx"),
        P(("ctx", "fsdp")),
        P(("ctx", "fsdp"), None),
        P(("ctx", "fsdp"), None),
        P(("ctx", "fsdp")),
        P(("ctx", "fsdp"), None),
        P(None, ("ctx", "fsdp")),
        P("fsdp", "ctx", None),
    )
    out_specs = (
        P("fsdp", "ctx", None),
        P("fsdp", "ctx", None),
        P(("ctx", "fsdp"), None),
        P(("ctx", "fsdp"), None),
        P(("ctx", "fsdp"), None),
        P(None, ("ctx", "fsdp")),
        P(("ctx", "fsdp")),
        P(("ctx", "fsdp")),
    )
    step = functools.partial(body, mesh.shape["ctx"], mesh.shape["fsdp"])
    return jax.shard_map(step, mesh=mesh, in_specs=in_specs, out_specs=out_specs, check_vma=False)
```

time: 766 us -> 537 us (0.70)
  waiting for transfers between devices: 600 us -> 292 us
  blocking collectives: 0 us -> 58.3 us
  local copies, waits for them, and re-layouts: 27.3 us -> 63.9 us
  Pallas kernels: 44.1 us -> 19.4 us
  starting transfers between devices: 0.65 us -> 19.5 us
    reduce_scatter x3 -> x1, waiting for transfers between devices: 360 us -> 104 us  [body(): lax.psum_scatter(jnp.concatenate([jnp.einsum('td,te->de', attended, resid...]
    all_gather x2 -> x1, waiting for transfers between devices: 135 us -> 50.1 us  [body(): lax.all_gather(jnp.concatenate([inputs[0], seg_block], axis=0), 'ctx', ax...]
    all_to_all x0 -> x3, waiting for transfers between devices: none -> 76.4 us  [the longest x1 36 us: body(): lax.all_to_all(row_grad_normed.astype(jnp.bfloat16).reshape(ctx_size, tok...]
    all_to_all x0 -> x2, blocking collectives: none -> 58.3 us  [the longest x1 44 us: body(): lax.all_to_all(qkv_terms, everyone, 0, 0, tiled=True)]
    all_gather x1, waiting for transfers between devices: 105 us -> 61.1 us  [body(): rest_full = lax.all_gather(rest_own, everyone, axis=0, tiled=True)]
    concatenate x2, local copies, waits for them, and re-layouts: 1.77 us -> 30.6 us  [the longest x1 30.1 us: body(): jnp.concatenate([jnp.einsum('td,te->de', attended, residual_half, preferr...]
    pallas_call x2, Pallas kernels: 44.1 us -> 19.4 us  [the longest x1 9.85 us: attend(): pl.pallas_call(lambda *refs: attend_kernel(scale, *refs), grid=(heads, ro...]
    all_to_all x0 -> x3, starting transfers between devices: none -> 19.4 us  [the longest x1 8.15 us: body(): lax.all_to_all(row_grad_normed.astype(jnp.bfloat16).reshape(ctx_size, tok...]
  transfers between devices with their start and end apart: 6 -> 6, of which waited for: 6 -> 6; matrix products, arithmetic and copies ran while one was open for 7% -> 8% of each run, Pallas kernels for 2% -> 4%
where the time goes in v2:
time: 537 us; the launch traced here: 535 us
  waiting for transfers between devices  292 us (54%)
  local copies, waits for them, and re-layouts  63.9 us (12%)
  blocking collectives  58.3 us (11%)
  matrix products  49.2 us (9%)
  starting transfers between devices  19.5 us (4%)
  Pallas kernels  19.4 us (4%)
  other arithmetic  18.4 us (3%)
  between operations  14.2 us (3%)
    reduce_scatter x1, waiting for transfers between devices, body(): lax.psum_scatter(jnp.concatenate([jnp.einsum('td,te->de', attended, resid...  104 us
    all_gather x1, waiting for transfers between devices, body(): rest_full = lax.all_gather(rest_own, everyone, axis=0, tiled=True)  61.1 us
    all_gather x1, waiting for transfers between devices, body(): lax.all_gather(jnp.concatenate([inputs[0], seg_block], axis=0), 'ctx', ax...  50.1 us
    all_to_all x1, blocking collectives, body(): lax.all_to_all(qkv_terms, everyone, 0, 0, tiled=True)  44 us
    all_to_all x1, waiting for transfers between devices, body(): lax.all_to_all(row_grad_normed.astype(jnp.bfloat16).reshape(ctx_size, tok...  36 us
    all_to_all x1, waiting for transfers between devices, body(): lax.all_to_all(qkv_parts, everyone, 0, 0, tiled=True)  35.3 us
    concatenate x1, local copies, waits for them, and re-layouts, body(): jnp.concatenate([jnp.einsum('td,te->de', attended, residual_half, preferr...  30.1 us
    all_to_all x1, blocking collectives, body(): lax.all_to_all(row_attended.reshape(own_width, row_count).T.reshape(ctx_s...  14.3 us
  transfers between devices with their start and end apart: 6, of which 6 were waited for; matrix products, arithmetic and copies ran while one was open for 8% of the time, Pallas kernels for 4%

profile of v2, /device:TPU:11, one launch (start us, length us, event | category | flops | bytes accessed | tf_op | source)
XLA Modules:
  0.0 535.0 jit_solution(17044977492763371652)
XLA Ops:
  8.0 1.7 fusion.73
  9.7 1.9 pad_maximum_fusion.3
  11.6 50.1 %all-gather.3.cloned.1.call-done = bf16[1152,1024]{1,0:T(8,128)(2,1)} async-done(((bf16[144,1024]{1,0:T(8,128)(2,1)}), bf16[1152,1024]{1,0:T(8,128)(2,1)}) %all-gather.3.cloned.1.call-update) | async-done | bytes 2359312 | tf_op jit(solution)/shard_map/all_gather | solution.py:196
  63.4 5.8 %all-to-all-start = ((bf16[32,32,512]{2,1,0:T(8,128)(2,1)}), bf16[32,32,512]{2,1,0:T(8,128)(2,1)}, u32[]{:S(2)}, u32[]{:S(2)}) async-start(bf16[32,32,512]{2,1,0:T(8,128)(2,1)} %bitcast.4), calls=%async_computation | async-start | bytes 2097152 | tf_op jit(solution)/shard_map/all_to_all | solution.py:210
  69.9 35.3 %all-to-all-done = bf16[32,32,512]{2,1,0:T(8,128)(2,1)} async-done(((bf16[32,32,512]{2,1,0:T(8,128)(2,1)}), bf16[32,32,512]{2,1,0:T(8,128)(2,1)}, u32[]{:S(2)}, u32[]{:S(2)}) %all-to-all-start) | async-done | bytes 1048608 | tf_op jit(solution)/shard_map/all_to_all | solution.py:210
  106.7 1.3 copy.66
  109.8 2.2 fusion.54
  116.7 9.9 %attend.1 = (bf16[2,64,1024]{2,1,0:T(8,128)(2,1)}, f32[2,1024,1]{2,1,0:T(8,128)}) custom-call(bf16[2,64,1024]{2,1,0:T(8,128)(2,1)} %get-tuple-element.41.refs_0_, bf16[2,64,1024]{2,1,0:T(8,128)(2,1)} %get-tuple-element.40.refs_1_, bf16[2,64,1024]{2,1,0:T(8,128)(2,1)} %bitcast.111, f32[1024,1]{1,0:T(8,128)} %copy.67.refs_3_, f32[1,1024]{1,0:T(1,128)} %bitcast.133), custom_call_target="tpu_custom_call" | custom-call | tf_op jit(solution)/shard_map/attend/pallas_call | solution.py:140
  127.7 14.3 %all_to_all.25 = bf16[8,128,128]{2,1,0:T(8,128)(2,1)S(1)} all-to-all(bf16[8,128,128]{2,1,0:T(8,128)(2,1)S(1)} %bitcast.122), channel_id=1, replica_groups=mesh['ctx'=8,'fsdp'=4] {'ctx'}, dimensions={0} | all-to-all | bytes 524288 | tf_op jit(solution)/shard_map/all_to_all | solution.py:243
  142.9 61.1 %all-gather.5.cloned.1.call-done = bf16[1024,8896]{1,0:T(8,128)(2,1)} async-done(((bf16[32,8896]{1,0:T(8,128)(2,1)}), bf16[1024,8896]{1,0:T(8,128)(2,1)}) %all-gather.5.cloned.1.call-update) | async-done | bytes 18219024 | tf_op jit(solution)/shard_map/all_gather | solution.py:220
  204.0 2.2 fusion.87
  206.5 5.8 %fusion.2 = f32[128,5248]{1,0:T(8,128)S(1)} fusion(bf16[1024,8896]{1,0:T(8,128)(2,1)} %all-gather.5.cloned.1.call-done, f32[128,1024]{1,0:T(8,128)S(1)} %get-tuple-element.57, f32[1024]{0:T(1024)S(1)} %get-tuple-element.27, f32[128]{0:T(128)S(1)} %add_rsqrt_fusion.2, f32[128]{0:T(128)S(1)} %broadcast_multiply_fusion.8), kind=kOutput, calls=%fused_computation.3 | convolution fusion | flops 1376256000 | bytes 13964288 | tf_op jit(solution)/shard_map/dot_general | solution.py:254
  212.2 6.1 %multiply_convert_fusion.2 = (bf16[128,2624]{1,0:T(8,128)(2,1)S(1)}, f32[128,2624]{1,0:T(8,128)S(1)}, bf16[128,2624]{1,0:T(8,128)(2,1)S(1)}) fusion(f32[128,5248]{1,0:T(8,128)S(1)} %fusion.2, bf16[1024,8896]{1,0:T(8,128)(2,1)} %all-gather.5.cloned.1.call-done, bf16[1,128,1024]{2,1,0:T(8,128)(2,1)S(1)} %copy-done.13), kind=kOutput, calls=%fused_computation.40 | convolution fusion | flops 713728000 | bytes 11141120 | tf_op jit(solution)/shard_map/td,df->tf/dot_general | solution.py:264
  219.6 5.9 %convolution_convert_fusion = bf16[1024,5248]{1,0:T(8,128)(2,1)} fusion(bf16[128,2624]{1,0:T(8,128)(2,1)S(1)} %get-tuple-element.29, bf16[128,2624]{1,0:T(8,128)(2,1)S(1)} %get-tuple-element.33, f32[128,1024]{1,0:T(8,128)S(1)} %get-tuple-element.57, f32[1024]{0:T(1024)S(1)} %get-tuple-element.27, f32[128]{0:T(128)S(1)} %add_rsqrt_fusion.2, ...), kind=kOutput, calls=%fused_computation | convolution fusion | flops 1384316928 | bytes 12620800 | tf_op jit(solution)/shard_map/td,tf->df/dot_general | solution.py:283
  225.5 6.5 %multiply_reduce_fusion.2 = (bf16[1024]{0:T(1024)(128)(2,1)S(1)}, f32[128]{0:T(128)S(1)}, f32[128]{0:T(128)S(1)}, f32[128,1024]{1,0:T(8,128)S(1)}) fusion(f32[128,1024]{1,0:T(8,128)S(1)} %get-tuple-element.57, f32[128]{0:T(128)S(1)} %add_rsqrt_fusion.2, f32[128]{0:T(128)S(1)} %broadcast_multiply_fusion.8, f32[1024]{0:T(1024)S(1)} %get-tuple-element.27, ...), kind=kOutput, calls=%fused_computation.98 | convolution fusion | flops 1379465984 | bytes 13148160 | tf_op jit(solution)/shard_map/tf,df->td/dot_general | solution.py:268
  234.1 2.1 convolution_convert_fusion.2
  236.2 3.9 copy.77
  240.1 5.1 fusion.4
  245.2 8.1 %copy.78 = bf16[1024,2624]{1,0:T(8,128)(2,1)} copy(bf16[1024,2624]{0,1:T(8,128)(2,1)} %fusion.4) | data formatting | bytes 10747904 | tf_op jit(solution)/shard_map/convert_element_type | solution.py:288
  253.3 30.1 %concatenate.48 = bf16[1024,9024]{1,0:T(8,128)(2,1)} concatenate(bf16[1024,1024]{1,0:T(8,128)(2,1)} %copy.77, bf16[1024,5248]{1,0:T(8,128)(2,1)} %convolution_convert_fusion, bf16[1024,2624]{1,0:T(8,128)(2,1)} %copy.78, bf16[1024,128]{1,0:T(8,128)(2,1)} %pad.20), dimensions={1} | concatenate | bytes 36962304 | tf_op jit(solution)/shard_map/concatenate | solution.py:278
  283.4 2.6 fusion.45
  286.8 5.4 %all-to-all-start.2 = ((bf16[8,128,128]{2,1,0:T(8,128)(2,1)}), bf16[8,128,128]{2,1,0:T(8,128)(2,1)}, u32[]{:S(2)}, u32[]{:S(2)}) async-start(bf16[8,128,128]{2,1,0:T(8,128)(2,1)} %bitcast.120), calls=%async_computation.2 | async-start | bytes 524288 | tf_op jit(solution)/shard_map/all_to_all | solution.py:300
  292.1 2.0 multiply_convert_fusion
  294.2 5.1 all-to-all-done.2
  299.3 1.8 copy.72
  301.1 9.5 %attend_grads.1 = (f32[2,64,1024]{2,1,0:T(8,128)}, f32[2,64,1024]{2,1,0:T(8,128)}, f32[2,64,1024]{2,1,0:T(8,128)}) custom-call(bf16[2,64,1024]{2,1,0:T(8,128)(2,1)} %get-tuple-element.41.refs_0_, bf16[2,64,1024]{2,1,0:T(8,128)(2,1)} %get-tuple-element.40.refs_1_, bf16[2,64,1024]{2,1,0:T(8,128)(2,1)} %bitcast.112, f32[1024,1]{1,0:T(8,128)} %copy.67.refs_3_, ...), custom_call_target="tpu_custom_call" | custom-call | tf_op jit(solution)/shard_map/attend_grads/pallas_call | solution.py:160
  314.4 4.2 multiply_reduce_fusion
  320.3 44.0 %all_to_all.26 = bf16[32,32,512]{2,1,0:T(8,128)(2,1)} all-to-all(bf16[32,32,512]{2,1,0:T(8,128)(2,1)S(1)} %bitcast.110), channel_id=1, replica_groups=mesh['ctx'=8,'fsdp'=4] {'ctx','fsdp'}, dimensions={0} | all-to-all | bytes 2097152 | tf_op jit(solution)/shard_map/all_to_all | solution.py:357
  364.3 8.2 %all-to-all-start.3 = ((bf16[8,128,1024]{2,1,0:T(8,128)(2,1)}), bf16[8,128,1024]{2,1,0:T(8,128)(2,1)S(1)}, u32[]{:S(2)}, u32[]{:S(2)}) async-start(bf16[8,128,1024]{2,1,0:T(8,128)(2,1)} %bitcast.117), calls=%async_computation.3 | async-start | bytes 4194304 | tf_op jit(solution)/shard_map/all_to_all | solution.py:338
  372.8 5.6 %fusion.48 = bf16[1,128,1024]{2,1,0:T(8,128)(2,1)} fusion(f32[128,1024]{1,0:T(8,128)S(1)} %get-tuple-element.57, bf16[128,2624]{1,0:T(8,128)(2,1)} %multiply_convert_fusion.3, bf16[1024,8896]{1,0:T(8,128)(2,1)} %all-gather.5.cloned.1.call-done), kind=kOutput, calls=%fused_computation.63 | convolution fusion | flops 688128000 | bytes 6979584 | tf_op jit(solution)/shard_map/tf,df->td/dot_general | solution.py:261
  382.3 36.0 %all-to-all-done.3 = bf16[8,128,1024]{2,1,0:T(8,128)(2,1)S(1)} async-done(((bf16[8,128,1024]{2,1,0:T(8,128)(2,1)}), bf16[8,128,1024]{2,1,0:T(8,128)(2,1)S(1)}, u32[]{:S(2)}, u32[]{:S(2)}) %all-to-all-start.3) | async-done | bytes 2097184 | tf_op jit(solution)/shard_map/all_to_all | solution.py:338
  419.8 104.4 %reduce-scatter.2.cloned.1.call-done = bf16[32,9024]{1,0:T(8,128)(2,1)} async-done(((bf16[1024,9024]{1,0:T(8,128)(2,1)}), bf16[32,9024]{1,0:T(8,128)(2,1)}) %reduce-scatter.2.cloned.1.call-update) | async-done | bytes 577552 | tf_op jit(solution)/shard_map/reduce_scatter | solution.py:277
  (112 shorter events, 32.6 us)
Async XLA Ops:
  7.2 54.6 %copy-start.17 = (bf16[32]{0:T(256)(128)(2,1)S(1)}, bf16[32]{0:T(256)(128)(2,1)}, u32[]{:S(2)}) copy-start(bf16[32]{0:T(256)(128)(2,1)} %param.14) | copy-start | bytes 196
  7.2 54.6 %copy-start.18 = (bf16[32]{0:T(256)(128)(2,1)S(1)}, bf16[32]{0:T(256)(128)(2,1)}, u32[]{:S(2)}) copy-start(bf16[32]{0:T(256)(128)(2,1)} %param.11) | copy-start | bytes 196
  7.2 54.7 %copy-start.15 = (bf16[32,3072]{1,0:T(8,128)(2,1)S(1)}, bf16[32,3072]{1,0:T(8,128)(2,1)}, u32[]{:S(2)}) copy-start(bf16[32,3072]{1,0:T(8,128)(2,1)} %param.12) | copy-start | bytes 589828
  7.2 54.5 %all-gather.3.cloned.1.call-start = ((), (), s32[]{:S(2)}) async-start(), calls=%async_computation.6 | async-start | bytes 2654208 | tf_op jit(solution)/shard_map/all_gather | solution.py:196
  9.7 194.3 %all-gather.5.cloned.1.call-start = ((), (), s32[]{:S(2)}) async-start(), calls=%async_computation.7 | async-start | bytes 18923520 | tf_op jit(solution)/shard_map/all_gather | solution.py:220
  63.4 41.8 %all-to-all-start = ((bf16[32,32,512]{2,1,0:T(8,128)(2,1)}), bf16[32,32,512]{2,1,0:T(8,128)(2,1)}, u32[]{:S(2)}, u32[]{:S(2)}) async-start(bf16[32,32,512]{2,1,0:T(8,128)(2,1)} %bitcast.4), calls=%async_computation | async-start | bytes 2097152 | tf_op jit(solution)/shard_map/all_to_all | solution.py:210
  69.2 455.1 %reduce-scatter.2.cloned.1.call-start = ((), (), s32[]{:S(2)}) async-start(), calls=%async_computation.8 | async-start | bytes 19193856 | tf_op jit(solution)/shard_map/reduce_scatter | solution.py:277
  69.8 36.9 %copy-start = (bf16[1152,1024]{1,0:T(8,128)(2,1)S(1)}, bf16[1152,1024]{1,0:T(8,128)(2,1)}, u32[]{:S(2)}) copy-start(bf16[1152,1024]{1,0:T(8,128)(2,1)} %all-gather.3.cloned.1.call-done) | copy-start | bytes 7077892
  69.9 45.8 %copy-start.6 = (f32[64,1024]{1,0:T(8,128)}, f32[64,1024]{1,0:T(8,128)S(1)}, u32[]{:S(2)}) copy-start(f32[64,1024]{1,0:T(8,128)S(1)} %get-tuple-element.60) | copy-start | bytes 786436
  112.0 1.2 copy-start.12
  113.2 2.4 copy-start.16
  116.7 87.3 %copy-start.1 = (bf16[1,128,1024]{2,1,0:T(8,128)(2,1)S(1)}, bf16[1,128,1024]{2,1,0:T(8,128)(2,1)}, u32[]{:S(2)}) copy-start(bf16[1,128,1024]{2,1,0:T(8,128)(2,1)} %param.9) | copy-start | bytes 786436
  206.5 5.8 %copy-start.13 = (bf16[1,128,1024]{2,1,0:T(8,128)(2,1)S(1)}, bf16[1,128,1024]{2,1,0:T(8,128)(2,1)}, u32[]{:S(2)}) copy-start(bf16[1,128,1024]{2,1,0:T(8,128)(2,1)} %param.17) | copy-start | bytes 786436
  232.0 2.1 copy-start.8
  233.3 0.8 copy-start.2
  286.8 12.5 %all-to-all-start.2 = ((bf16[8,128,128]{2,1,0:T(8,128)(2,1)}), bf16[8,128,128]{2,1,0:T(8,128)(2,1)}, u32[]{:S(2)}, u32[]{:S(2)}) async-start(bf16[8,128,128]{2,1,0:T(8,128)(2,1)} %bitcast.120), calls=%async_computation.2 | async-start | bytes 524288 | tf_op jit(solution)/shard_map/all_to_all | solution.py:300
  311.9 1.0 copy-start.7
  311.9 1.1 copy-start.10
  312.0 1.3 copy-start.11
  313.2 1.0 copy-start.14
  314.4 4.2 copy-start.9
  364.3 53.9 %all-to-all-start.3 = ((bf16[8,128,1024]{2,1,0:T(8,128)(2,1)}), bf16[8,128,1024]{2,1,0:T(8,128)(2,1)S(1)}, u32[]{:S(2)}, u32[]{:S(2)}) async-start(bf16[8,128,1024]{2,1,0:T(8,128)(2,1)} %bitcast.117), calls=%async_computation.3 | async-start | bytes 4194304 | tf_op jit(solution)/shard_map/all_to_all | solution.py:338
  372.8 5.6 %copy-start.4 = (bf16[32,32,512]{2,1,0:T(8,128)(2,1)S(1)}, bf16[32,32,512]{2,1,0:T(8,128)(2,1)}, u32[]{:S(2)}) copy-start(bf16[32,32,512]{2,1,0:T(8,128)(2,1)} %all_to_all.26) | copy-start | bytes 3145732
  382.3 36.6 %copy-start.3 = (f32[128,1024]{1,0:T(8,128)S(1)}, f32[128,1024]{1,0:T(8,128)}, u32[]{:S(2)}) copy-start(f32[128,1024]{1,0:T(8,128)} %copy-done.2) | copy-start | bytes 1572868
  524.3 2.7 copy-start.5
Sparse Core Ops, SparseCore 0:
  10.8 50.9 all-gather.2
  65.2 138.7 all-gather.4
  283.5 240.7 reduce-scatter.1

commit v3 on v2

--- a/solution.py
+++ b/solution.py
@@ -165,6 +165,38 @@
         out_shape=[grads, grads, grads],
         name="attend_grads",
     )(query_cols, key_cols, value_cols, seg_col, seg_row, log_total, grad_cols, attended_cols)
+
+
+def weight_grads_kernel(bounds, *refs):
+    gain_ref, out_ref = refs[-2:]
+    for i in range(3):
+        out_ref[:, bounds[i] : bounds[i] + refs[2 * i + 1].shape[1]] = lax.dot_general(
+            refs[2 * i][...],
+            refs[2 * i + 1][...],
+            (((0,), (0,)), ((), ())),
+            preferred_element_type=jnp.float32,
+        ).astype(jnp.bfloat16)
+    out_ref[:, bounds[3] : bounds[3] + LANES] = gain_ref[...]
+
+
+def weight_grads(pairs, gain_block, bounds, total):
+    tok_count, width = pairs[0][0].shape
+    rows = min(LANES, width)
+    in_specs = []
+    operands = []
+    for left, right in pairs:
+        in_specs.append(pl.BlockSpec((tok_count, rows), lambda r: (0, r)))
+        in_specs.append(pl.BlockSpec(right.shape, lambda r: (0, 0)))
+        operands += [left, right]
+    in_specs.append(pl.BlockSpec((rows, LANES), lambda r: (r, 0)))
+    return pl.pallas_call(
+        lambda *refs: weight_grads_kernel(bounds, *refs),
+        grid=(width // rows,),
+        in_specs=in_specs,
+        out_specs=pl.BlockSpec((rows, total), lambda r: (r, 0)),
+        out_shape=jax.ShapeDtypeStruct((width, total), jnp.bfloat16),
+        name="weight_grads",
+    )(*operands, gain_block)
 
 
 def body(
@@ -193,9 +225,16 @@
     weight_rows = w_qkv.shape[0]
 
     seg_block = jnp.pad(segment_ids.astype(jnp.bfloat16), ((0, SEG_ROWS - 1), (0, width - tok_count)))
-    gathered = lax.all_gather(
-        jnp.concatenate([inputs[0], seg_block], axis=0), "ctx", axis=0, tiled=True
-    ).reshape(ctx_size, tok_count + SEG_ROWS, width)
+    gathered = lax.all_to_all(
+        jnp.broadcast_to(
+            jnp.concatenate([inputs[0], seg_block], axis=0),
+            (ctx_size, tok_count + SEG_ROWS, width),
+        ),
+        "ctx",
+        0,
+        0,
+        tiled=True,
+    )
 
     qkv_parts = jnp.transpose(
         w_qkv.reshape(weight_rows, 3, ctx_size, own_width), (2, 0, 1, 3)
@@ -216,7 +255,6 @@
     gain_second = gains[1]
 
     rest_own = jnp.concatenate([w_out_attn, w_in, w_out_mlp.T], axis=1)
-    rest_own, gathered = lax.optimization_barrier((rest_own, gathered))
     rest_full = lax.all_gather(rest_own, everyone, axis=0, tiled=True)
     attn_full = rest_full[:, :width]
     in_full = rest_full[:, width : width + 2 * hidden_units]
@@ -275,20 +313,15 @@
     residual_half = grad_residual.astype(jnp.bfloat16)
     gain_block = jnp.pad(grad_gain_two[:, None], ((0, 0), (0, LANES - 1))).astype(jnp.bfloat16)
     weight_sums = lax.psum_scatter(
-        jnp.concatenate(
-            [
-                jnp.einsum(
-                    "td,te->de", attended, residual_half, preferred_element_type=jnp.float32
-                ).astype(jnp.bfloat16),
-                jnp.einsum(
-                    "td,tf->df", normed_mlp, grad_expanded, preferred_element_type=jnp.float32
-                ).astype(jnp.bfloat16),
-                jnp.einsum(
-                    "td,tf->df", grad_out, product, preferred_element_type=jnp.float32
-                ).astype(jnp.bfloat16),
-                gain_block,
-            ],
-            axis=1,
+        weight_grads(
+            (
+                (attended, residual_half),
+                (normed_mlp, grad_expanded),
+                (grad_out, product),
+            ),
+            gain_block,
+            (0, width, width + 2 * hidden_units + LANES, width + 2 * hidden_units),
+            width + 3 * hidden_units + LANES,
         ),
         everyone,
         scatter_dimension=0,
@@ -368,8 +401,8 @@
     ).astype(jnp.bfloat16)
     grad_attn_rows = weight_sums[:, :width]
     grad_in_rows = weight_sums[:, width : width + 2 * hidden_units]
-    grad_mlp_cols = weight_sums[:, width + 2 * hidden_units : width + 3 * hidden_units].T
-    gain_sum_two = weight_sums[:, width + 3 * hidden_units]
+    grad_mlp_cols = weight_sums[:, width + 2 * hidden_units + LANES :].T
+    gain_sum_two = weight_sums[:, width + 2 * hidden_units]
     return (
         block_out[None],
         grad_tokens[None],

time: 537 us -> 488 us (0.909)
  local copies, waits for them, and re-layouts: 63.9 us -> 23.7 us
  matrix products: 49.2 us -> 34 us
  Pallas kernels: 19.4 us -> 31 us
  waiting for transfers between devices: 292 us -> 281 us
  starting transfers between devices: 19.5 us -> 26.1 us
    all_to_all x0 -> x1, waiting for transfers between devices: none -> 96.5 us  [body(): lax.all_to_all(jnp.broadcast_to(jnp.concatenate([inputs[0], seg_block], a...]
    all_gather x1, waiting for transfers between devices: 61.1 us -> 0.01 us  [body(): rest_full = lax.all_gather(rest_own, everyone, axis=0, tiled=True)]
    all_gather x1 -> x0, waiting for transfers between devices: 50.1 us -> none  [body(): lax.all_gather(jnp.concatenate([inputs[0], seg_block], axis=0), 'ctx', ax...]
    concatenate x1 -> x0, local copies, waits for them, and re-layouts: 30.1 us -> none  [body(): jnp.concatenate([jnp.einsum('td,te->de', attended, residual_half, preferr...]
    dot_general x3 -> x0, matrix products: 13 us -> none  [the longest x1 5.88 us: body(): jnp.einsum('td,tf->df', normed_mlp, grad_expanded, preferred_element_type...]
    convert_element_type x2 -> x0, local copies, waits for them, and re-layouts: 12.1 us -> none  [body(): weight_sums = lax.psum_scatter(jnp.concatenate([jnp.einsum('td,te->de', a...]
    pallas_call x0 -> x1, Pallas kernels: none -> 11.6 us  [weight_grads(): pl.pallas_call(lambda *refs: weight_grads_kernel(bounds, *refs), grid=(wi...]
    all_to_all x0 -> x1, starting transfers between devices: none -> 5.82 us  [body(): lax.all_to_all(jnp.broadcast_to(jnp.concatenate([inputs[0], seg_block], a...]
  transfers between devices with their start and end apart: 6 -> 6, of which waited for: 6 -> 5; matrix products, arithmetic and copies ran while one was open for 8% -> 8% of each run, Pallas kernels for 4% -> 4%
where the time goes in v3:
time: 488 us; the launch traced here: 486 us
  waiting for transfers between devices  281 us (58%)
  blocking collectives  58.7 us (12%)
  matrix products  34 us (7%)
  Pallas kernels  31 us (6%)
  starting transfers between devices  26.1 us (5%)
  local copies, waits for them, and re-layouts  23.7 us (5%)
  other arithmetic  17.5 us (4%)
  between operations  14.6 us (3%)
    reduce_scatter x1, waiting for transfers between devices, body(): lax.psum_scatter(weight_grads(((attended, residual_half), (normed_mlp, gr...  106 us
    all_to_all x1, waiting for transfers between devices, body(): lax.all_to_all(jnp.broadcast_to(jnp.concatenate([inputs[0], seg_block], a...  96.5 us
    all_to_all x1, blocking collectives, body(): lax.all_to_all(qkv_terms, everyone, 0, 0, tiled=True)  44.8 us
    all_to_all x1, waiting for transfers between devices, body(): lax.all_to_all(row_grad_normed.astype(jnp.bfloat16).reshape(ctx_size, tok...  36 us
    all_to_all x1, waiting for transfers between devices, body(): lax.all_to_all(qkv_parts, everyone, 0, 0, tiled=True)  35.8 us
    all_to_all x1, blocking collectives, body(): lax.all_to_all(row_attended.reshape(own_width, row_count).T.reshape(ctx_s...  13.9 us
    pallas_call x1, Pallas kernels, weight_grads(): pl.pallas_call(lambda *refs: weight_grads_kernel(bounds, *refs), grid=(wi...  11.6 us
    pallas_call x1, Pallas kernels, attend(): pl.pallas_call(lambda *refs: attend_kernel(scale, *refs), grid=(heads, ro...  9.86 us
  transfers between devices with their start and end apart: 6, of which 5 were waited for; matrix products, arithmetic and copies ran while one was open for 8% of the time, Pallas kernels for 4%

profile of v3, /device:TPU:11, one launch (start us, length us, event | category | flops | bytes accessed | tf_op | source)
XLA Modules:
  0.0 486.2 jit_solution(13479057995040597754)
XLA Ops:
  7.2 2.0 pad_maximum_fusion.1
  10.9 6.3 %all-to-all-start = ((bf16[32,32,512]{2,1,0:T(8,128)(2,1)}), bf16[32,32,512]{2,1,0:T(8,128)(2,1)S(1)}, u32[]{:S(2)}, u32[]{:S(2)}) async-start(bf16[32,32,512]{2,1,0:T(8,128)(2,1)} %bitcast.4), calls=%async_computation | async-start | bytes 2097152 | tf_op jit(solution)/shard_map/all_to_all | solution.py:249
  17.2 35.8 %all-to-all-done = bf16[32,32,512]{2,1,0:T(8,128)(2,1)S(1)} async-done(((bf16[32,32,512]{2,1,0:T(8,128)(2,1)}), bf16[32,32,512]{2,1,0:T(8,128)(2,1)S(1)}, u32[]{:S(2)}, u32[]{:S(2)}) %all-to-all-start) | async-done | bytes 1048608 | tf_op jit(solution)/shard_map/all_to_all | solution.py:249
  53.1 1.7 broadcast_in_dim.18
  54.8 5.8 %all-to-all-start.1 = ((bf16[8,144,1024]{2,1,0:T(8,128)(2,1)}), bf16[8,144,1024]{2,1,0:T(8,128)(2,1)S(1)}, u32[]{:S(2)}, u32[]{:S(2)}) async-start(bf16[8,144,1024]{2,1,0:T(8,128)(2,1)} %broadcast_in_dim.18), calls=%async_computation.1 | async-start | bytes 4718592 | tf_op jit(solution)/shard_map/all_to_all | solution.py:228
  62.9 96.5 %all-to-all-done.1 = bf16[8,144,1024]{2,1,0:T(8,128)(2,1)S(1)} async-done(((bf16[8,144,1024]{2,1,0:T(8,128)(2,1)}), bf16[8,144,1024]{2,1,0:T(8,128)(2,1)S(1)}, u32[]{:S(2)}, u32[]{:S(2)}) %all-to-all-start.1) | async-done | bytes 2359328 | tf_op jit(solution)/shard_map/all_to_all | solution.py:228
  162.7 1.1 copy-done.13
  165.7 1.4 fusion.79
  168.3 9.9 %attend.1 = (bf16[2,64,1024]{2,1,0:T(8,128)(2,1)}, f32[2,1024,1]{2,1,0:T(8,128)}) custom-call(bf16[2,64,1024]{2,1,0:T(8,128)(2,1)} %get-tuple-element.39.refs_0_, bf16[2,64,1024]{2,1,0:T(8,128)(2,1)} %get-tuple-element.38.refs_1_, bf16[2,64,1024]{2,1,0:T(8,128)(2,1)} %bitcast.111, f32[1024,1]{1,0:T(8,128)} %copy.77.refs_3_, f32[1,1024]{1,0:T(1,128)} %bitcast.134), custom_call_target="tpu_custom_call" | custom-call | tf_op jit(solution)/shard_map/attend/pallas_call | solution.py:140
  179.3 13.9 %all_to_all.30 = bf16[8,128,128]{2,1,0:T(8,128)(2,1)S(1)} all-to-all(bf16[8,128,128]{2,1,0:T(8,128)(2,1)S(1)} %bitcast.123), channel_id=1, replica_groups=mesh['ctx'=8,'fsdp'=4] {'ctx'}, dimensions={0} | all-to-all | bytes 524288 | tf_op jit(solution)/shard_map/all_to_all | solution.py:281
  194.6 2.2 fusion.82
  197.3 5.8 %fusion.2 = f32[128,5248]{1,0:T(8,128)S(1)} fusion(bf16[128,1024]{1,0:T(8,128)(2,1)S(1)} %multiply_convert_fusion.4.refs_2_, bf16[1024,8896]{1,0:T(8,128)(2,1)} %all-gather.2.cloned.1.call-done), kind=kOutput, calls=%fused_computation.2 | convolution fusion | flops 1375731712 | bytes 13697024 | tf_op jit(solution)/shard_map/dot_general | solution.py:292
  203.1 6.1 %multiply_convert_fusion.2 = (bf16[128,2624]{1,0:T(8,128)(2,1)S(1)}, f32[128,2624]{1,0:T(8,128)S(1)}, bf16[128,2624]{1,0:T(8,128)(2,1)S(1)}) fusion(f32[128,5248]{1,0:T(8,128)S(1)} %fusion.2, bf16[1024,8896]{1,0:T(8,128)(2,1)} %all-gather.2.cloned.1.call-done, bf16[1,128,1024]{2,1,0:T(8,128)(2,1)S(1)} %copy-done.14), kind=kOutput, calls=%fused_computation.36 | convolution fusion | flops 713728000 | bytes 11141120 | tf_op jit(solution)/shard_map/td,df->tf/dot_general | solution.py:302
  209.2 1.3 multiply_convert_fusion.3.refs_5_
  210.8 7.0 %multiply_reduce_fusion.2 = (bf16[1024]{0:T(1024)(128)(2,1)S(1)}, f32[128]{0:T(128)S(1)}, f32[128]{0:T(128)S(1)}, f32[128,1024]{1,0:T(8,128)S(1)}) fusion(f32[128,1024]{1,0:T(8,128)S(1)} %get-tuple-element.55, f32[128]{0:T(128)S(1)} %add_rsqrt_fusion.2, f32[128]{0:T(128)S(1)} %broadcast_multiply_fusion.8, f32[1024]{0:T(1024)S(1)} %get-tuple-element.23, ...), kind=kOutput, calls=%fused_computation.94 | convolution fusion | flops 1376779008 | bytes 13148160 | tf_op jit(solution)/shard_map/tf,df->td/dot_general | solution.py:306
  218.8 1.1 fusion.77
  219.9 11.6 %weight_grads.1 = bf16[1024,9024]{1,0:T(8,128)(2,1)} custom-call(bf16[128,1024]{1,0:T(8,128)(2,1)} %copy_bitcast_fusion.1.refs_0_, bf16[128,1024]{1,0:T(8,128)(2,1)} %get-tuple-element.25.refs_1_, bf16[128,1024]{1,0:T(8,128)(2,1)} %copy-done.15, bf16[128,5248]{1,0:T(8,128)(2,1)} %copy-done.1, bf16[128,1024]{1,0:T(8,128)(2,1)} %bitcast.120, ...), custom_call_target="tpu_custom_call" | custom-call | tf_op jit(solution)/shard_map/weight_grads/pallas_call | solution.py:192
  231.5 2.5 fusion.44
  234.8 6.1 %all-to-all-start.3 = ((bf16[8,128,128]{2,1,0:T(8,128)(2,1)}), bf16[8,128,128]{2,1,0:T(8,128)(2,1)}, u32[]{:S(2)}, u32[]{:S(2)}) async-start(bf16[8,128,128]{2,1,0:T(8,128)(2,1)} %bitcast.122), calls=%async_computation.3 | async-start | bytes 524288 | tf_op jit(solution)/shard_map/all_to_all | solution.py:333
  240.9 2.0 multiply_convert_fusion
  242.9 5.9 %all-to-all-done.3 = bf16[8,128,128]{2,1,0:T(8,128)(2,1)} async-done(((bf16[8,128,128]{2,1,0:T(8,128)(2,1)}), bf16[8,128,128]{2,1,0:T(8,128)(2,1)}, u32[]{:S(2)}, u32[]{:S(2)}) %all-to-all-start.3) | async-done | bytes 262176 | tf_op jit(solution)/shard_map/all_to_all | solution.py:333
  248.9 1.8 copy.82
  250.6 9.5 %attend_grads.1 = (f32[2,64,1024]{2,1,0:T(8,128)}, f32[2,64,1024]{2,1,0:T(8,128)}, f32[2,64,1024]{2,1,0:T(8,128)}) custom-call(bf16[2,64,1024]{2,1,0:T(8,128)(2,1)} %get-tuple-element.39.refs_0_, bf16[2,64,1024]{2,1,0:T(8,128)(2,1)} %get-tuple-element.38.refs_1_, bf16[2,64,1024]{2,1,0:T(8,128)(2,1)} %bitcast.112, f32[1024,1]{1,0:T(8,128)} %copy.77.refs_3_, ...), custom_call_target="tpu_custom_call" | custom-call | tf_op jit(solution)/shard_map/attend_grads/pallas_call | solution.py:160
  260.2 1.3 broadcast_multiply_fusion.1
  264.3 2.9 multiply_reduce_fusion
  268.8 44.8 %all_to_all.31 = bf16[32,32,512]{2,1,0:T(8,128)(2,1)} all-to-all(bf16[32,32,512]{2,1,0:T(8,128)(2,1)S(1)} %bitcast.110), channel_id=1, replica_groups=mesh['ctx'=8,'fsdp'=4] {'ctx','fsdp'}, dimensions={0} | all-to-all | bytes 2097152 | tf_op jit(solution)/shard_map/all_to_all | solution.py:390
  313.7 7.9 %all-to-all-start.4 = ((bf16[8,128,1024]{2,1,0:T(8,128)(2,1)}), bf16[8,128,1024]{2,1,0:T(8,128)(2,1)S(1)}, u32[]{:S(2)}, u32[]{:S(2)}) async-start(bf16[8,128,1024]{2,1,0:T(8,128)(2,1)} %bitcast.115), calls=%async_computation.4 | async-start | bytes 4194304 | tf_op jit(solution)/shard_map/all_to_all | solution.py:371
  321.9 5.6 %fusion.47 = bf16[1,128,1024]{2,1,0:T(8,128)(2,1)} fusion(f32[128,1024]{1,0:T(8,128)S(1)} %get-tuple-element.55, bf16[128,2624]{1,0:T(8,128)(2,1)} %multiply_convert_fusion.3.refs_5_, bf16[1024,8896]{1,0:T(8,128)(2,1)} %all-gather.2.cloned.1.call-done), kind=kOutput, calls=%fused_computation.59 | convolution fusion | flops 688128000 | bytes 6979584 | tf_op jit(solution)/shard_map/tf,df->td/dot_general | solution.py:299
  328.7 1.3 copy.85
  331.4 36.0 %all-to-all-done.4 = bf16[8,128,1024]{2,1,0:T(8,128)(2,1)S(1)} async-done(((bf16[8,128,1024]{2,1,0:T(8,128)(2,1)}), bf16[8,128,1024]{2,1,0:T(8,128)(2,1)S(1)}, u32[]{:S(2)}, u32[]{:S(2)}) %all-to-all-start.4) | async-done | bytes 2097184 | tf_op jit(solution)/shard_map/all_to_all | solution.py:371
  369.0 106.2 %reduce-scatter.2.cloned.1.call-done = bf16[32,9024]{1,0:T(8,128)(2,1)} async-done(((bf16[1024,9024]{1,0:T(8,128)(2,1)}), bf16[32,9024]{1,0:T(8,128)(2,1)}) %reduce-scatter.2.cloned.1.call-update) | async-done | bytes 577552 | tf_op jit(solution)/shard_map/reduce_scatter | solution.py:315
  475.2 1.2 convert_element_type.150
  (117 shorter events, 27.0 us)
Async XLA Ops:
  7.2 2.1 copy-start.20
  7.2 2.1 copy-start.21
  7.2 2.2 copy-start.18
  7.2 187.4 %all-gather.2.cloned.1.call-start = ((), (), s32[]{:S(2)}) async-start(), calls=%async_computation.7 | async-start | bytes 18923520 | tf_op jit(solution)/shard_map/all_gather | solution.py:258
  10.9 6.3 %copy-start.22 = (s32[1,128]{1,0:T(1,128)S(1)}, s32[1,128]{1,0:T(1,128)}, u32[]{:S(2)}) copy-start(s32[1,128]{1,0:T(1,128)} %param.10) | copy-start | bytes 1540
  10.9 6.3 %copy-start = (bf16[1,128,1024]{2,1,0:T(8,128)(2,1)S(1)}, bf16[1,128,1024]{2,1,0:T(8,128)(2,1)}, u32[]{:S(2)}) copy-start(bf16[1,128,1024]{2,1,0:T(8,128)(2,1)} %param.9) | copy-start | bytes 786436
  10.9 42.2 %all-to-all-start = ((bf16[32,32,512]{2,1,0:T(8,128)(2,1)}), bf16[32,32,512]{2,1,0:T(8,128)(2,1)S(1)}, u32[]{:S(2)}, u32[]{:S(2)}) async-start(bf16[32,32,512]{2,1,0:T(8,128)(2,1)} %bitcast.4), calls=%async_computation | async-start | bytes 2097152 | tf_op jit(solution)/shard_map/all_to_all | solution.py:249
  53.1 1.8 copy-start.10
  54.8 104.6 %all-to-all-start.1 = ((bf16[8,144,1024]{2,1,0:T(8,128)(2,1)}), bf16[8,144,1024]{2,1,0:T(8,128)(2,1)S(1)}, u32[]{:S(2)}, u32[]{:S(2)}) async-start(bf16[8,144,1024]{2,1,0:T(8,128)(2,1)} %broadcast_in_dim.18), calls=%async_computation.1 | async-start | bytes 4718592 | tf_op jit(solution)/shard_map/all_to_all | solution.py:228
  60.6 414.5 %reduce-scatter.2.cloned.1.call-start = ((), (), s32[]{:S(2)}) async-start(), calls=%async_computation.8 | async-start | bytes 19193856 | tf_op jit(solution)/shard_map/reduce_scatter | solution.py:315
  61.3 106.0 %copy-start.4 = (f32[64,1024]{1,0:T(8,128)}, f32[64,1024]{1,0:T(8,128)S(1)}, u32[]{:S(2)}) copy-start(f32[64,1024]{1,0:T(8,128)S(1)} %get-tuple-element.58) | copy-start | bytes 786436
  160.5 1.2 copy-start.11
  162.7 1.2 copy-start.13
  164.6 2.6 copy-start.19
  193.2 0.7 copy-start.16
  197.2 5.8 %copy-start.15 = (bf16[128,1024]{1,0:T(8,128)(2,1)}, bf16[128,1024]{1,0:T(8,128)(2,1)S(1)}, u32[]{:S(2)}) copy-start(bf16[128,1024]{1,0:T(8,128)(2,1)S(1)} %multiply_convert_fusion.4.refs_2_) | copy-start | bytes 786436
  197.3 5.8 %copy-start.14 = (bf16[1,128,1024]{2,1,0:T(8,128)(2,1)S(1)}, bf16[1,128,1024]{2,1,0:T(8,128)(2,1)}, u32[]{:S(2)}) copy-start(bf16[1,128,1024]{2,1,0:T(8,128)(2,1)} %param.17) | copy-start | bytes 786436
  210.8 7.0 %copy-start.1 = (bf16[128,5248]{1,0:T(8,128)(2,1)}, bf16[128,5248]{1,0:T(8,128)(2,1)S(1)}, u32[]{:S(2)}) copy-start(bf16[128,5248]{1,0:T(8,128)(2,1)S(1)} %pad_maximum_fusion.refs_3_) | copy-start | bytes 4030468
  234.8 14.0 %all-to-all-start.3 = ((bf16[8,128,128]{2,1,0:T(8,128)(2,1)}), bf16[8,128,128]{2,1,0:T(8,128)(2,1)}, u32[]{:S(2)}, u32[]{:S(2)}) async-start(bf16[8,128,128]{2,1,0:T(8,128)(2,1)} %bitcast.122), calls=%async_computation.3 | async-start | bytes 524288 | tf_op jit(solution)/shard_map/all_to_all | solution.py:333
  261.5 1.0 copy-start.5
  261.5 1.1 copy-start.8
  261.5 1.3 copy-start.9
  262.8 1.1 copy-start.17
  263.0 1.3 copy-start.12
  264.3 2.9 copy-start.6
  313.7 53.7 %all-to-all-start.4 = ((bf16[8,128,1024]{2,1,0:T(8,128)(2,1)}), bf16[8,128,1024]{2,1,0:T(8,128)(2,1)S(1)}, u32[]{:S(2)}, u32[]{:S(2)}) async-start(bf16[8,128,1024]{2,1,0:T(8,128)(2,1)} %bitcast.115), calls=%async_computation.4 | async-start | bytes 4194304 | tf_op jit(solution)/shard_map/all_to_all | solution.py:371
  321.9 5.6 %copy-start.2 = (bf16[32,32,512]{2,1,0:T(8,128)(2,1)S(1)}, bf16[32,32,512]{2,1,0:T(8,128)(2,1)}, u32[]{:S(2)}) copy-start(bf16[32,32,512]{2,1,0:T(8,128)(2,1)} %all_to_all.31) | copy-start | bytes 3145732
  331.4 36.6 %copy-start.7 = (f32[128,1024]{1,0:T(8,128)S(1)}, f32[128,1024]{1,0:T(8,128)}, u32[]{:S(2)}) copy-start(f32[128,1024]{1,0:T(8,128)} %get-tuple-element.26) | copy-start | bytes 1572868
  475.2 2.6 copy-start.3
Sparse Core Ops, SparseCore 0:
  11.5 169.8 all-gather.1
  231.7 243.4 reduce-scatter.1
